TPU v7x, 32 devices: a whole 2x2x4 slice. The times are simulated.
32 devices in a mesh: seq: 8 (over z, y), head: 4 (over x, core).
Axes of the slice: x: 2, y: 2, z: 4, core: 2. Of those that a mesh axis runs over, the one named last changes fastest.
Arguments:
- x_in: bfloat16 [1024, 8192], P('seq', 'head'), may hold values from -6 to 6
- bc_in: bfloat16 [1024, 2, 128], P('seq'), may hold values from -0.59765625 to 0.59765625
- conv_x: bfloat16 [4, 8192], P(None, 'head'), may hold values from -3 to 3
- conv_bc: bfloat16 [4, 2, 128], replicated, may hold values from -3 to 3
- log_decay: float32 [1024, 64], P('seq', 'head'), may hold values from -2 to 0, as said below
- skip: float32 [64], P('head'), may hold values from 0.5 to 1.5
- queries: bfloat16 [1024, 8192], P('seq', 'head'), may hold values from -12 to 12
- keys: bfloat16 [1024, 1024], P('seq', 'head'), may hold values from -5 to 5
- values: bfloat16 [1024, 1024], P('seq', 'head'), may hold values from -6 to 6
- d_mixed: bfloat16 [1024, 8192], P('seq', 'head'), may hold values from -6 to 6
Outputs:
- mixed: bfloat16 [1024, 8192], P('seq', 'head')
- d_queries: float32 [1024, 8192], P('seq', 'head')
- d_keys: float32 [1024, 1024], P('seq', 'head')
- d_values: float32 [1024, 1024], P('seq', 'head')
- d_x_in: float32 [1024, 8192], P('seq', 'head')
- d_bc_in: float32 [1024, 2, 128], P('seq')
- d_log_decay: float32 [1024, 64], P('seq', 'head')
Inputs may be any that keep to these rules, and one draw needn't show every extreme that they name: `log_decay`: every entry is negative.
All inputs are finite; a program needn't handle non-finite values.
Results may differ from a plain program's by a relative error of at most 0.012.
The roundings to bfloat16 on the way count: a program that leaves them out, or rounds other values in their place, can miss the bound.
Values may be sent and summed in bfloat16 or wider, within the bound.
A program may use at most 128 MiB of HBM per device.

v0:
```python
import math

import jax
import jax.numpy as jnp
from jax import lax
from jax.sharding import PartitionSpec as P

SSM_DIM = 128
HEAD_DIM = 128


masked_value = -1e30
highest_precision = lax.Precision.HIGHEST


def from_behind(block, axis, distance):
    devices = range(lax.axis_size(axis))
    route = [(i - distance, i) for i in devices if i - distance in devices]
    return lax.ppermute(block, axis, route)


def carried_in(value, axis, join, neutral, backward):
    count, mine = (lax.axis_size(axis), lax.axis_index(axis))
    pieces = jax.tree.map(lambda part: lax.all_gather(part, axis), value)
    if backward:
        pieces = jax.tree.map(lambda part: part[::-1], pieces)
        mine = count - 1 - mine
    running = jax.tree.map(
        lambda part, zero: jnp.full_like(part, 0) + jnp.asarray(zero, part.dtype), value, neutral
    )

    def lap(position, running):
        longer = join(running, jax.tree.map(lambda part: part[position], pieces))
        return jax.tree.map(lambda new, old: jnp.where(position < mine, new, old), longer, running)

    return lax.fori_loop(0, count - 1, lap, running)


def silu_slope(pre):
    sigmoid = jax.nn.sigmoid(pre)
    return sigmoid * (1.0 + pre * (1.0 - sigmoid))


def conv_forward(inputs, before, weight):
    padded = jnp.concatenate([before, inputs], axis=0)
    length = inputs.shape[0]
    total = jnp.zeros(inputs.shape, jnp.float32)
    for tap in range(weight.shape[0]):
        total = total + weight[tap].astype(jnp.float32) * padded[tap : tap + length].astype(
            jnp.float32
        )
    return total


def conv_backward(grads, after, weight):
    width = weight.shape[0]
    padded = jnp.concatenate([grads, after], axis=0)
    length = grads.shape[0]
    total = jnp.zeros(grads.shape, jnp.float32)
    for tap in range(width):
        offset = width - 1 - tap
        total = total + weight[tap].astype(jnp.float32) * padded[offset : offset + length]
    return total


def span_step(state, x_blk, b_blk, c_blk, a_blk, skip):
    size = x_blk.shape[0]
    running = jnp.cumsum(a_blk, axis=0)
    gaps = running[:, None, :] - running[None, :, :]
    order = jnp.arange(size, dtype=jnp.int32)
    allowed = (order[:, None] >= order[None, :])[:, :, None]
    fading = jnp.exp(jnp.where(allowed, gaps, masked_value))
    inner = jnp.dot(c_blk, b_blk.T, precision=highest_precision)
    outputs = jnp.einsum(
        "tsh,shp->thp", inner[:, :, None] * fading, x_blk, precision=highest_precision
    )
    carried = jnp.einsum("tn,hpn->thp", c_blk, state, precision=highest_precision)
    outputs = outputs + jnp.exp(running)[:, :, None] * carried + skip[None, :, None] * x_blk
    final = running[-1]
    tail_fade = jnp.exp(final[None, :] - running)
    state = jnp.exp(final)[:, None, None] * state + jnp.einsum(
        "sh,shp,sn->hpn", tail_fade, x_blk, b_blk, precision=highest_precision
    )
    return (outputs, state)


def local_ssd(x_rows, b_rows, c_rows, decay, state, skip):
    outputs, state = span_step(state, x_rows, b_rows, c_rows, decay, skip)
    pieces = [outputs]
    return (jnp.concatenate(pieces, axis=0), state)


def link(earlier, later):
    return (earlier[0] * later[0], later[0][:, None, None] * earlier[1] + later[1])


def block_scores(query_tile_block, key_tile_block, pos_q, pos_k, softmax_scale):
    attention_scores = (
        jnp.einsum(
            "ajuk,pjk->juap", query_tile_block, key_tile_block, preferred_element_type=jnp.float32
        )
        * softmax_scale
    )
    allowed = pos_k[None, :] <= pos_q[:, None]
    return jnp.where(allowed, attention_scores, masked_value)


def block_grads(
    query_tile_block,
    gradient_block,
    lse_blk,
    delta_blk,
    pos_q,
    key_tile_block,
    value_tile_block,
    pos_k,
    softmax_scale,
):
    attention_scores = block_scores(query_tile_block, key_tile_block, pos_q, pos_k, softmax_scale)
    probs = jnp.exp(attention_scores - lse_blk[..., None])
    attention_weights = probs.astype(jnp.bfloat16)
    weight_gradient = jnp.einsum(
        "ajuk,pjk->juap", gradient_block, value_tile_block, preferred_element_type=jnp.float32
    )
    score_gradient = (probs * (weight_gradient - delta_blk[..., None])).astype(jnp.bfloat16)
    return (attention_weights, score_gradient)


def shards(x_in, bc_in, conv_x, conv_bc, log_decay, skip, queries, keys, values, d_mixed):
    tok_rows = x_in.shape[0]
    edge = conv_x.shape[0] - 1
    seq_index = lax.axis_index("seq")
    tail_x, tail_bc = from_behind((x_in[tok_rows - edge :], bc_in[tok_rows - edge :]), "seq", 1)
    pre_x = conv_forward(x_in, tail_x, conv_x)
    pre_bc = conv_forward(bc_in, tail_bc, conv_bc)
    x_conv = jax.nn.silu(pre_x).astype(jnp.bfloat16)
    bc_conv = jax.nn.silu(pre_bc).astype(jnp.bfloat16)
    ssm_heads = x_in.shape[1] // SSM_DIM
    x_rows = x_conv.astype(jnp.float32).reshape(tok_rows, ssm_heads, SSM_DIM)
    b_rows = bc_conv[:, 0].astype(jnp.float32)
    c_rows = bc_conv[:, 1].astype(jnp.float32)
    running = jnp.cumsum(log_decay, axis=0)
    overall = running[-1]
    carry_decay = jnp.exp(overall)
    own_state = jnp.einsum(
        "sh,shp,sn->hpn",
        jnp.exp(overall[None, :] - running),
        x_rows,
        b_rows,
        precision=highest_precision,
    )
    neutral = (jnp.ones_like(carry_decay), jnp.zeros_like(own_state))
    _, state_in = carried_in((carry_decay, own_state), "seq", link, neutral, False)

    def ssd_part(x_arg, b_arg, c_arg, decay_arg, state_arg):
        return local_ssd(x_arg, b_arg, c_arg, decay_arg, state_arg, skip)

    (ssm_out, _), ssd_back = jax.vjp(ssd_part, x_rows, b_rows, c_rows, log_decay, state_in)
    kv_heads = keys.shape[1] // HEAD_DIM
    query_heads = queries.shape[1] // HEAD_DIM
    ratio = query_heads // kv_heads
    softmax_scale = HEAD_DIM ** (-0.5)
    query_quartet = queries.reshape(tok_rows, kv_heads, ratio, HEAD_DIM)
    gradient_quartet = d_mixed.reshape(tok_rows, kv_heads, ratio, HEAD_DIM)
    full_keys, full_values = (
        lax.all_gather(keys, "seq", axis=0, tiled=True),
        lax.all_gather(values, "seq", axis=0, tiled=True),
    )
    length = full_keys.shape[0]
    blk_size = math.gcd(512, length)
    first = seq_index * tok_rows
    pos_q = first + jnp.arange(tok_rows, dtype=jnp.int32)
    blk_count = (first + tok_rows + blk_size - 1) // blk_size

    def key_block(index):
        begin = index * blk_size
        key_tile_block = lax.dynamic_slice_in_dim(full_keys, begin, blk_size, 0).reshape(
            blk_size, kv_heads, HEAD_DIM
        )
        value_tile_block = lax.dynamic_slice_in_dim(full_values, begin, blk_size, 0).reshape(
            blk_size, kv_heads, HEAD_DIM
        )
        pos_k = begin + jnp.arange(blk_size, dtype=jnp.int32)
        return (key_tile_block, value_tile_block, pos_k)

    def max_step(index, carry):
        top, total = carry
        key_tile_block, _, pos_k = key_block(index)
        attention_scores = block_scores(query_quartet, key_tile_block, pos_q, pos_k, softmax_scale)
        new_top = jnp.maximum(top, jnp.max(attention_scores, axis=-1))
        total = total * jnp.exp(top - new_top) + jnp.sum(
            jnp.exp(attention_scores - new_top[..., None]), axis=-1
        )
        return (new_top, total)

    stat_shape = (kv_heads, ratio, tok_rows)
    top, total = lax.fori_loop(
        0,
        blk_count,
        max_step,
        (jnp.full(stat_shape, masked_value, jnp.float32), jnp.zeros(stat_shape, jnp.float32)),
    )
    lse = top + jnp.log(total)

    def out_step(index, acc):
        key_tile_block, value_tile_block, pos_k = key_block(index)
        attention_scores = block_scores(query_quartet, key_tile_block, pos_q, pos_k, softmax_scale)
        attention_weights = jnp.exp(attention_scores - lse[..., None]).astype(jnp.bfloat16)
        return acc + jnp.einsum(
            "mxlo,oma->lmxa",
            attention_weights,
            value_tile_block,
            preferred_element_type=jnp.float32,
        )

    attended_output = lax.fori_loop(
        0, blk_count, out_step, jnp.zeros((tok_rows, kv_heads, ratio, HEAD_DIM), jnp.float32)
    )
    mixed = (ssm_out.reshape(tok_rows, -1) + attended_output.reshape(tok_rows, -1)).astype(
        jnp.bfloat16
    )
    delta_terms = jnp.einsum(
        "qwns,qwns->wnq",
        gradient_quartet.astype(jnp.float32),
        attended_output,
        precision=highest_precision,
    )

    def grad_step(index, carry):
        dquery, key_terms, value_terms = carry
        key_tile_block, value_tile_block, pos_k = key_block(index)
        attention_weights, score_gradient = block_grads(
            query_quartet,
            gradient_quartet,
            lse,
            delta_terms,
            pos_q,
            key_tile_block,
            value_tile_block,
            pos_k,
            softmax_scale,
        )
        dquery = dquery + jnp.einsum(
            "mxlo,oma->lmxa", score_gradient, key_tile_block, preferred_element_type=jnp.float32
        )
        dkey = (
            jnp.einsum(
                "aznl,naze->lae", score_gradient, query_quartet, preferred_element_type=jnp.float32
            )
            * softmax_scale
        )
        value_gradient = jnp.einsum(
            "aznl,naze->lae",
            attention_weights,
            gradient_quartet,
            preferred_element_type=jnp.float32,
        )
        key_terms = lax.dynamic_update_slice_in_dim(
            key_terms, dkey.reshape(blk_size, -1), index * blk_size, 0
        )
        value_terms = lax.dynamic_update_slice_in_dim(
            value_terms, value_gradient.reshape(blk_size, -1), index * blk_size, 0
        )
        return (dquery, key_terms, value_terms)

    term_shape = (length, kv_heads * HEAD_DIM)
    start_carry = (
        jnp.zeros(query_quartet.shape, jnp.float32),
        jnp.zeros(term_shape, jnp.float32),
        jnp.zeros(term_shape, jnp.float32),
    )
    dquery, key_terms, value_terms = lax.fori_loop(0, blk_count, grad_step, start_carry)
    d_keys, d_values = (
        lax.psum_scatter(key_terms, "seq", scatter_dimension=0, tiled=True),
        lax.psum_scatter(value_terms, "seq", scatter_dimension=0, tiled=True),
    )
    d_queries = (dquery * softmax_scale).reshape(tok_rows, -1)
    grad_y = d_mixed.astype(jnp.float32).reshape(tok_rows, ssm_heads, SSM_DIM)
    own_grad = jnp.einsum(
        "th,thp,tn->hpn", jnp.exp(running), grad_y, c_rows, precision=highest_precision
    )
    _, state_grad = carried_in((carry_decay, own_grad), "seq", link, neutral, True)
    grad_x, grad_b, grad_c, d_log_decay, _ = ssd_back((grad_y, state_grad))
    group_grad = lax.psum(jnp.stack([grad_b, grad_c], axis=1), "head")
    grad_pre_x = grad_x.reshape(tok_rows, -1) * silu_slope(pre_x)
    grad_pre_bc = group_grad * silu_slope(pre_bc)
    after_x, after_bc = from_behind((grad_pre_x[:edge], grad_pre_bc[:edge]), "seq", -1)
    d_x_in = conv_backward(grad_pre_x, after_x, conv_x)
    d_bc_in = conv_backward(grad_pre_bc, after_bc, conv_bc)
    return (mixed, d_queries, d_keys, d_values, d_x_in, d_bc_in, d_log_decay)


def solution(mesh):
    in_specs = (
        P("seq", "head"),
        P("seq", None, None),
        P(None, "head"),
        P(),
        P("seq", "head"),
        P("head"),
        P("seq", "head"),
        P("seq", "head"),
        P("seq", "head"),
        P("seq", "head"),
    )
    out_specs = (
        P("seq", "head"),
        P("seq", "head"),
        P("seq", "head"),
        P("seq", "head"),
        P("seq", "head"),
        P("seq", None, None),
        P("seq", "head"),
    )
    return jax.shard_map(shards, mesh=mesh, in_specs=in_specs, out_specs=out_specs, check_vma=False)
```

profile of v0, /device:TPU:0, one launch (start us, length us, event | category | flops | bytes accessed | tf_op | source)
XLA Modules:
  0.0 500.9 jit_solution(5619813644991056389)
XLA Ops:
  8.1 4.9 collective-permute-start.1
  14.8 2.1 copy.162
  17.6 2.7 fusion.35
  20.4 3.4 collective-permute-start
  24.0 18.0 %all-gather.2 = f32[8,1,16]{2,1,0:T(1,128)S(1)} all-gather(f32[1,1,16]{2,1,0:T(1,128)S(1)} %get-tuple-element.630), channel_id=1, replica_groups=mesh['seq'=8,'head'=4] {'seq'}, dimensions={0}, use_global_device_ids=true | all-gather | bytes 576 | tf_op jit(solution)/shard_map/all_gather | solution.py:24
  42.0 1.6 multiply_convert_fusion
  43.9 101.9 %all-gather.8.cloned.1.call-done = f32[128,128,128]{2,1,0:T(8,128)} async-done(((f32[16,128,128]{2,1,0:T(8,128)}), f32[128,128,128]{2,1,0:T(8,128)}) %all-gather.8.cloned.1.call-update) | async-done | bytes 8388624 | tf_op jit(solution)/shard_map/all_gather | solution.py:24
  145.8 7.7 %rev.7 = f32[8,16,128,128]{3,2,1,0:T(8,128)} reverse(f32[8,16,128,128]{3,2,1,0:T(8,128)} %bitcast.294), dimensions={0} | reverse | bytes 16777216 | tf_op jit(solution)/shard_map/rev | solution.py:26
  153.6 10.5 %while.71 = (s32[]{:T(128)}, f32[16,128,128]{2,1,0:T(8,128)S(1)}, s32[]{:T(128)}, f32[8,16]{1,0:T(8,128)S(1)}, f32[8,16,128,128]{3,2,1,0:T(8,128)}, /*index=5*/s32[]{:T(128)}, s32[]{:T(128)}) while((s32[]{:T(128)}, f32[16,128,128]{2,1,0:T(8,128)S(1)}, s32[]{:T(128)}, f32[8,16]{1,0:T(8,128)S(1)}, f32[8,16,128,128]{3,2,1,0:T(8,128)}, ...), condition=%wide.region_14.15_spmd.clone, body=%wide.region_13.14_spmd.clone.sunk | while | flops 1048580 | bytes 3146025 | solution.py:36
  153.7 1.5 fusion.176
  155.2 1.5 fusion.176
  156.7 1.5 fusion.176
  158.2 1.5 fusion.176
  161.1 1.5 fusion.176
  164.2 1.6 fusion.47
  166.5 1.6 fusion.33
  171.1 31.5 %all_gather.28 = bf16[1024,256]{0,1:T(8,128)(2,1)S(1)} all-gather(bf16[128,256]{0,1:T(8,128)(2,1)S(1)} %copy.156), channel_id=1, replica_groups=mesh['seq'=8,'head'=4] {'seq'}, dimensions={0}, use_global_device_ids=true | all-gather | bytes 589824 | tf_op jit(solution)/shard_map/all_gather | solution.py:166
  202.6 3.0 while.67
  202.8 1.9 fusion.155
  206.3 34.4 %all_gather.27 = bf16[1024,256]{0,1:T(8,128)(2,1)} all-gather(bf16[128,256]{0,1:T(8,128)(2,1)S(1)} %copy.155), channel_id=1, replica_groups=mesh['seq'=8,'head'=4] {'seq'}, dimensions={0}, use_global_device_ids=true | all-gather | bytes 589824 | tf_op jit(solution)/shard_map/all_gather | solution.py:167
  241.8 5.8 %while.68 = (s32[]{:T(128)}, f32[128,2,8,128]{0,3,2,1:T(8,128)}, s32[]{:T(128)}, bf16[1024,256]{0,1:T(8,128)(2,1)}, bf16[1024,256]{0,1:T(8,128)(2,1)S(1)}, /*ind...) while((s32[]{:T(128)}, f32[128,2,8,128]{0,3,2,1:T(8,128)}, ...), condition=%wide.region_8.9_spmd.clone, body=%wide.region_7.8_spmd.clone.sunk | while | flops 541393536 | bytes 4338863 | solution.py:216
  241.8 1.7 constant_dynamic-slice_fusion.10
  243.6 4.0 fusion.159
  247.6 2.1 multiply_reduce_fusion
  251.3 2.7 fusion.55
  254.0 1.8 fusion.37
  256.0 48.6 %all-gather.6.cloned.1.call-done = f32[128,128,128]{2,1,0:T(8,128)} async-done(((f32[16,128,128]{2,1,0:T(8,128)}), f32[128,128,128]{2,1,0:T(8,128)}) %all-gather.6.cloned.1.call-update) | async-done | bytes 8388624 | tf_op jit(solution)/shard_map/all_gather | solution.py:24
  304.7 15.1 %while.70 = (s32[]{:T(128)}, f32[16,128,128]{2,1,0:T(8,128)S(1)}, s32[]{:T(128)}, f32[8,16]{1,0:T(8,128)}, f32[8,16,128,128]{3,2,1,0:T(8,128)}, /*index=5*/s32[]{:T(128)}, s32[]{:T(128)}) while((s32[]{:T(128)}, f32[16,128,128]{2,1,0:T(8,128)S(1)}, s32[]{:T(128)}, f32[8,16]{1,0:T(8,128)}, f32[8,16,128,128]{3,2,1,0:T(8,128)}, ...), condition=%wide.region_2.3_spmd.clone, body=%wide.region_1.2_spmd.clone.sunk | while | flops 1048580 | bytes 3146025 | solution.py:36
  319.8 3.3 fusion.36
  327.3 19.0 %while.69 = (s32[]{:T(128)}, f32[128,2,8,128]{0,3,2,1:T(8,128)}, f32[1024,256]{1,0:T(8,128)}, f32[1024,256]{1,0:T(8,128)}, s32[]{:T(128)}, /*index=5*/bf16[1024,...) while((s32[]{:T(128)}, f32[128,2,8,128]{0,3,2,1:T(8,128)}, ...), condition=%wide.region_10.11_spmd.clone, body=%wide.region_9.10_spmd.clone.sunk | while | flops 1353122432 | bytes 51410276 | solution.py:272
  329.5 2.7 fusion.171
  332.1 1.6 fusion.174
  335.0 4.3 fusion.173
  339.3 2.0 copy.234
  341.3 2.1 constant_dynamic-update-slice_fusion.3
  343.5 2.8 fusion.172
  346.9 4.1 fusion.29
  351.0 2.6 copy.168
  353.6 1.7 multiply_multiply_fusion
  355.3 1.5 collective-permute-start.2
  359.3 2.6 copy.210
  364.2 2.7 fusion.49
  367.7 3.3 fusion.31
  371.0 2.6 copy.161
  373.9 2.1 add_convert_fusion
  381.1 2.1 collective-permute-done.3
  384.1 43.9 %reduce-scatter.3.cloned.1.call-done = f32[128,256]{1,0:T(8,128)} async-done(((f32[1024,256]{1,0:T(8,128)}), f32[128,256]{1,0:T(8,128)}) %reduce-scatter.3.cloned.1.call-update) | async-done | bytes 131088 | tf_op jit(solution)/shard_map/reduce_scatter | solution.py:274
  428.0 66.4 %reduce-scatter.5.cloned.1.call-done = f32[128,256]{1,0:T(8,128)} async-done(((f32[1024,256]{1,0:T(8,128)}), f32[128,256]{1,0:T(8,128)}) %reduce-scatter.5.cloned.1.call-update) | async-done | bytes 131088 | tf_op jit(solution)/shard_map/reduce_scatter | solution.py:275
  (227 shorter events, 49.8 us)
Async XLA Ops:
  7.2 13.2 %copy-start.23 = (bf16[128,2048]{1,0:T(8,128)(2,1)S(1)}, bf16[128,2048]{1,0:T(8,128)(2,1)}, u32[]{:S(2)}) copy-start(bf16[128,2048]{1,0:T(8,128)(2,1)} %param.20) | copy-start | bytes 1572868
  7.2 16.7 %copy-start.44 = (bf16[4,2048]{1,0:T(4,128)(2,1)S(1)}, bf16[4,2048]{1,0:T(4,128)(2,1)}, u32[]{:S(2)}) copy-start(bf16[4,2048]{1,0:T(4,128)(2,1)} %param.22) | copy-start | bytes 49156
  7.2 138.6 %all-gather.8.cloned.1.call-start = ((), (), s32[]{:S(2)}) async-start(), calls=%async_computation.6 | async-start | bytes 9437184 | tf_op jit(solution)/shard_map/all_gather | solution.py:24
  8.1 8.7 %collective-permute-start.1 = (bf16[3,2,128]{2,0,1:T(4,128)(2,1)S(1)}, bf16[3,2,128]{2,0,1:T(4,128)(2,1)S(1)}, u32[]{:S(2)}, u32[]{:S(2)}) collective-permute-start(bf16[3,2,128]{2,0,1:T(4,128)(2,1)S(1)} %slice.121), channel_id=1, source_target_pairs={{0,4},{4,8},{8,12},{12,16},{16,20},{20,24},{24,28},{1,5},{5,9},{9,... | collective-permute-start | bytes 4616 | tf_op jit(solution)/shard_map/ppermute | solution.py:19
  13.7 139.8 %copy-start.46 = (f32[2,128]{1,0:T(2,128)}, f32[2,128]{1,0:T(2,128)S(1)}, u32[]{:S(2)}) copy-start(f32[2,128]{1,0:T(2,128)S(1)} %get-tuple-element.635) | copy-start | bytes 3076
  13.7 139.8 %copy-start.48 = (f32[2,128]{1,0:T(2,128)}, f32[2,128]{1,0:T(2,128)S(1)}, u32[]{:S(2)}) copy-start(f32[2,128]{1,0:T(2,128)S(1)} %get-tuple-element.636) | copy-start | bytes 3076
  13.7 139.8 %copy-start.50 = (f32[2,128]{1,0:T(2,128)}, f32[2,128]{1,0:T(2,128)S(1)}, u32[]{:S(2)}) copy-start(f32[2,128]{1,0:T(2,128)S(1)} %get-tuple-element.637) | copy-start | bytes 3076
  13.7 139.8 %copy-start.52 = (f32[2,128]{1,0:T(2,128)}, f32[2,128]{1,0:T(2,128)S(1)}, u32[]{:S(2)}) copy-start(f32[2,128]{1,0:T(2,128)S(1)} %get-tuple-element.638) | copy-start | bytes 3076
  14.8 138.8 %copy-start.29 = (f32[128,16]{0,1:T(8,128)}, f32[128,16]{0,1:T(8,128)S(1)}, u32[]{:S(2)}) copy-start(f32[128,16]{0,1:T(8,128)S(1)} %copy.153) | copy-start | bytes 24580
  17.6 148.9 %copy-start.16 = (bf16[128,2,128]{2,0,1:T(8,128)(2,1)}, bf16[128,2,128]{2,0,1:T(8,128)(2,1)S(1)}, u32[]{:S(2)}) copy-start(bf16[128,2,128]{2,0,1:T(8,128)(2,1)S(1)} %get-tuple-element.619) | copy-start | bytes 196612
  20.3 284.4 %all-gather.6.cloned.1.call-start = ((), (), s32[]{:S(2)}) async-start(), calls=%async_computation.5 | async-start | bytes 9437184 | tf_op jit(solution)/shard_map/all_gather | solution.py:24
  20.4 21.6 %collective-permute-start = (bf16[3,2048]{1,0:T(4,128)(2,1)S(1)}, bf16[3,2048]{1,0:T(4,128)(2,1)S(1)}, u32[]{:S(2)}, u32[]{:S(2)}) collective-permute-start(bf16[3,2048]{1,0:T(4,128)(2,1)S(1)} %slice.91), channel_id=1, source_target_pairs={{0,4},{4,8},{8,12},{12,16},{16,20},{20,24},{24,28},{1,5},{5,9},{9,... | collective-permute-start | bytes 36872 | tf_op jit(solution)/shard_map/ppermute | solution.py:19
  23.9 129.7 %copy-start.33 = (f32[1,2048]{1,0:T(1,128)}, f32[1,2048]{1,0:T(1,128)S(1)}, u32[]{:S(2)}) copy-start(f32[1,2048]{1,0:T(1,128)S(1)} %get-tuple-element.631) | copy-start | bytes 24580
  23.9 129.7 %copy-start.35 = (f32[1,2048]{1,0:T(1,128)}, f32[1,2048]{1,0:T(1,128)S(1)}, u32[]{:S(2)}) copy-start(f32[1,2048]{1,0:T(1,128)S(1)} %get-tuple-element.632) | copy-start | bytes 24580
  23.9 129.7 %copy-start.37 = (f32[1,2048]{1,0:T(1,128)}, f32[1,2048]{1,0:T(1,128)S(1)}, u32[]{:S(2)}) copy-start(f32[1,2048]{1,0:T(1,128)S(1)} %get-tuple-element.633) | copy-start | bytes 24580
  23.9 129.7 %copy-start.39 = (f32[1,2048]{1,0:T(1,128)}, f32[1,2048]{1,0:T(1,128)S(1)}, u32[]{:S(2)}) copy-start(f32[1,2048]{1,0:T(1,128)S(1)} %get-tuple-element.634) | copy-start | bytes 24580
  42.0 111.6 %copy-start.45 = (f32[8,1,16]{2,1,0:T(1,128)}, f32[8,1,16]{2,1,0:T(1,128)S(1)}, u32[]{:S(2)}) copy-start(f32[8,1,16]{2,1,0:T(1,128)S(1)} %all-gather.2) | copy-start | bytes 1540
  43.9 122.6 %copy-start.9 = (bf16[128,2048]{0,1:T(8,128)(2,1)}, bf16[128,2048]{0,1:T(8,128)(2,1)S(1)}, u32[]{:S(2)}) copy-start(bf16[128,2048]{0,1:T(8,128)(2,1)S(1)} %copy.144) | copy-start | bytes 1572868
  164.1 89.9 %copy-start.3 = (f32[16,128,128]{2,1,0:T(8,128)}, f32[16,128,128]{2,1,0:T(8,128)S(1)}, u32[]{:S(2)}) copy-start(f32[16,128,128]{2,1,0:T(8,128)S(1)} %get-tuple-element.349) | copy-start | bytes 3145732
  168.2 207.9 %all-reduce.3.cloned.1.call-start = ((), (), s32[]{:S(2)}) async-start(), calls=%async_computation.4 | async-start | bytes 262144 | tf_op jit(solution)/shard_map/psum | solution.py:284
  241.8 9.6 %copy-start.31 = (f32[128,16]{0,1:T(8,128)S(1)}, f32[128,16]{0,1:T(8,128)}, u32[]{:S(2)}) copy-start(f32[128,16]{0,1:T(8,128)} %copy.150) | copy-start | bytes 24580
  247.6 8.2 %copy-start.17 = (bf16[128,2,128]{2,0,1:T(8,128)(2,1)S(1)}, bf16[128,2,128]{2,0,1:T(8,128)(2,1)}, u32[]{:S(2)}) copy-start(bf16[128,2,128]{2,0,1:T(8,128)(2,1)} %copy-done.16) | copy-start | bytes 196612
  304.7 15.2 %copy-start.30 = (f32[128,16]{0,1:T(8,128)S(1)}, f32[128,16]{0,1:T(8,128)}, u32[]{:S(2)}) copy-start(f32[128,16]{0,1:T(8,128)} %copy-done.29) | copy-start | bytes 24580
  319.8 7.5 %copy-start.1 = (f32[16,128,128]{2,1,0:T(8,128)}, f32[16,128,128]{2,1,0:T(8,128)S(1)}, u32[]{:S(2)}) copy-start(f32[16,128,128]{2,1,0:T(8,128)S(1)} %get-tuple-element.342) | copy-start | bytes 3145732
  324.0 103.9 %reduce-scatter.3.cloned.1.call-start = ((), (), s32[]{:S(2)}) async-start(), calls=%async_computation.2 | async-start | bytes 1179648 | tf_op jit(solution)/shard_map/reduce_scatter | solution.py:274
  346.3 148.1 %reduce-scatter.5.cloned.1.call-start = ((), (), s32[]{:S(2)}) async-start(), calls=%async_computation.3 | async-start | bytes 1179648 | tf_op jit(solution)/shard_map/reduce_scatter | solution.py:275
  346.9 10.0 %copy-start.5 = (f32[128,2,8,128]{0,3,2,1:T(8,128)S(1)}, f32[128,2,8,128]{0,3,2,1:T(8,128)}, u32[]{:S(2)}) copy-start(f32[128,2,8,128]{0,3,2,1:T(8,128)} %get-tuple-element.346) | copy-start | bytes 3145732
  353.6 8.3 %copy-start.57 = (f32[128,16]{0,1:T(8,128)S(1)}, f32[128,16]{0,1:T(8,128)}, u32[]{:S(2)}) copy-start(f32[128,16]{0,1:T(8,128)} %get-tuple-element.540) | copy-start | bytes 24580
  353.6 8.4 %copy-start.56 = (f32[128,16]{0,1:T(8,128)S(1)}, f32[128,16]{0,1:T(8,128)}, u32[]{:S(2)}) copy-start(f32[128,16]{0,1:T(8,128)} %get-tuple-element.541) | copy-start | bytes 24580
  353.6 9.1 %copy-start.34 = (f32[1,2048]{1,0:T(1,128)S(1)}, f32[1,2048]{1,0:T(1,128)}, u32[]{:S(2)}) copy-start(f32[1,2048]{1,0:T(1,128)} %copy-done.33) | copy-start | bytes 24580
  353.6 9.1 %copy-start.36 = (f32[1,2048]{1,0:T(1,128)S(1)}, f32[1,2048]{1,0:T(1,128)}, u32[]{:S(2)}) copy-start(f32[1,2048]{1,0:T(1,128)} %copy-done.35) | copy-start | bytes 24580
  353.6 9.1 %copy-start.38 = (f32[1,2048]{1,0:T(1,128)S(1)}, f32[1,2048]{1,0:T(1,128)}, u32[]{:S(2)}) copy-start(f32[1,2048]{1,0:T(1,128)} %copy-done.37) | copy-start | bytes 24580
  353.6 9.1 %copy-start.40 = (f32[1,2048]{1,0:T(1,128)S(1)}, f32[1,2048]{1,0:T(1,128)}, u32[]{:S(2)}) copy-start(f32[1,2048]{1,0:T(1,128)} %copy-done.39) | copy-start | bytes 24580
  355.3 7.4 %collective-permute-start.2 = (f32[3,2048]{1,0:T(4,128)S(1)}, f32[3,2048]{1,0:T(4,128)S(1)}, u32[]{:S(2)}, u32[]{:S(2)}) collective-permute-start(f32[3,2048]{1,0:T(4,128)S(1)} %slice.129), channel_id=1, source_target_pairs={{4,0},{8,4},{12,8},{16,12},{20,16},{24,20},{28,24},{5,1},{9,5},{13... | collective-permute-start | bytes 73736 | tf_op jit(solution)/shard_map/ppermute | solution.py:19
  358.0 9.7 %copy-start.26 = (f32[128,128]{0,1:T(8,128)S(1)}, f32[128,128]{0,1:T(8,128)}, u32[]{:S(2)}) copy-start(f32[128,128]{0,1:T(8,128)} %copy-done.25) | copy-start | bytes 196612
  358.0 9.7 %copy-start.32 = (f32[128,16]{0,1:T(8,128)S(1)}, f32[128,16]{0,1:T(8,128)}, u32[]{:S(2)}) copy-start(f32[128,16]{0,1:T(8,128)} %copy.150) | copy-start | bytes 24580
  358.0 9.7 %copy-start.41 = (pred[128,128]{0,1:T(8,128)(4,1)S(1)}, pred[128,128]{0,1:T(8,128)(4,1)}, u32[]{:S(2)}) copy-start(pred[128,128]{0,1:T(8,128)(4,1)} %iota_compare_fusion) | copy-start | bytes 49156
  359.3 8.4 %copy-start.11 = (bf16[128,2048]{0,1:T(8,128)(2,1)S(1)}, bf16[128,2048]{0,1:T(8,128)(2,1)}, u32[]{:S(2)}) copy-start(bf16[128,2048]{0,1:T(8,128)(2,1)} %copy-done.9) | copy-start | bytes 1572868
  359.3 8.4 %copy-start.59 = (f32[16]{0:T(128)S(1)}, f32[16]{0:T(128)}, u32[]{:S(2)}) copy-start(f32[16]{0:T(128)} %param.25) | copy-start | bytes 196
  364.2 9.5 %copy-start.4 = (f32[16,128,128]{2,1,0:T(8,128)S(1)}, f32[16,128,128]{2,1,0:T(8,128)}, u32[]{:S(2)}) copy-start(f32[16,128,128]{2,1,0:T(8,128)} %copy-done.3) | copy-start | bytes 3145732
  364.2 9.7 %copy-start.58 = (f32[16]{0:T(128)S(1)}, f32[16]{0:T(128)}, u32[]{:S(2)}) copy-start(f32[16]{0:T(128)} %get-tuple-element.617) | copy-start | bytes 196
  371.0 7.4 %copy-start.20 = (f32[128,16]{1,0:T(8,128)S(1)}, f32[128,16]{1,0:T(8,128)}, u32[]{:S(2)}) copy-start(f32[128,16]{1,0:T(8,128)} %copy-done.19) | copy-start | bytes 24580
  371.0 7.4 %copy-start.22 = (f32[128,16]{1,0:T(8,128)S(1)}, f32[128,16]{1,0:T(8,128)}, u32[]{:S(2)}) copy-start(f32[128,16]{1,0:T(8,128)} %copy-done.21) | copy-start | bytes 24580
  371.0 12.2 %copy-start.47 = (f32[2,128]{1,0:T(2,128)S(1)}, f32[2,128]{1,0:T(2,128)}, u32[]{:S(2)}) copy-start(f32[2,128]{1,0:T(2,128)} %copy-done.46) | copy-start | bytes 3076
  371.0 12.2 %copy-start.49 = (f32[2,128]{1,0:T(2,128)S(1)}, f32[2,128]{1,0:T(2,128)}, u32[]{:S(2)}) copy-start(f32[2,128]{1,0:T(2,128)} %copy-done.48) | copy-start | bytes 3076
  371.0 12.2 %copy-start.51 = (f32[2,128]{1,0:T(2,128)S(1)}, f32[2,128]{1,0:T(2,128)}, u32[]{:S(2)}) copy-start(f32[2,128]{1,0:T(2,128)} %copy-done.50) | copy-start | bytes 3076
  371.0 12.2 %copy-start.53 = (f32[2,128]{1,0:T(2,128)S(1)}, f32[2,128]{1,0:T(2,128)}, u32[]{:S(2)}) copy-start(f32[2,128]{1,0:T(2,128)} %copy-done.52) | copy-start | bytes 3076
  377.1 6.1 %collective-permute-start.3 = (f32[3,2,128]{2,0,1:T(4,128)S(1)}, f32[3,2,128]{2,0,1:T(4,128)S(1)}, u32[]{:S(2)}, u32[]{:S(2)}) collective-permute-start(f32[3,2,128]{2,0,1:T(4,128)S(1)} %slice.134), channel_id=1, source_target_pairs={{4,0},{8,4},{12,8},{16,12},{20,16},{24,20},{28,24},{5,1},{9,5},{13... | collective-permute-start | bytes 9224 | tf_op jit(solution)/shard_map/ppermute | solution.py:19
  (21 other events, 94.0 us)
Sparse Core Ops, SparseCore 0:
  20.4 125.3 all-gather.7
  168.3 136.3 all-gather.5
  324.1 30.4 all-reduce.2
  358.8 69.0 reduce-scatter.2
  431.8 62.4 reduce-scatter.4
where the time goes:
time: 503 us; the launch traced here: 501 us
  waiting for transfers between devices  264 us (52%)
  blocking collectives  84 us (17%)
  local copies, waits for them, and re-layouts  44.8 us (9%)
  matrix products  43 us (9%)
  other arithmetic  39.3 us (8%)
  between operations  14.4 us (3%)
  starting transfers between devices  11.3 us (2%)
    all_gather x2, waiting for transfers between devices, carried_in(): pieces = jax.tree.map(lambda part: lax.all_gather(part, axis), value)  151 us
    reduce_scatter x1, waiting for transfers between devices, shards(): lax.psum_scatter(value_terms, 'seq', scatter_dimension=0, tiled=True)  66.4 us
    reduce_scatter x1, waiting for transfers between devices, shards(): lax.psum_scatter(key_terms, 'seq', scatter_dimension=0, tiled=True)  43.9 us
    all_gather x1, blocking collectives, shards(): lax.all_gather(values, 'seq', axis=0, tiled=True)  34.4 us
    all_gather x1, blocking collectives, shards(): lax.all_gather(keys, 'seq', axis=0, tiled=True)  31.5 us
    select_n x14, other arithmetic, lap(): jnp.where(position < mine, new, old)  20.4 us
    all_gather x1, blocking collectives, carried_in(): pieces = jax.tree.map(lambda part: lax.all_gather(part, axis), value)  18 us
    ppermute x4, starting transfers between devices, from_behind(): return lax.ppermute(block, axis, route)  11.1 us
  transfers between devices with their start and end apart: 9, of which 5 were waited for; matrix products, arithmetic and copies ran while one was open for 16% of the time, Pallas kernels for 0%

commit v1 on v0

v1 whole, which is shorter than its diff:
```python
import functools
import math

import jax
import jax.numpy as jnp
from jax import lax
from jax.experimental import pallas as pl
from jax.experimental.pallas import tpu as pltpu
from jax.sharding import PartitionSpec as P

D = 128
EDGE = 16
F32 = jnp.float32
BF16 = jnp.bfloat16
MESH = pl.DeviceIdType.MESH
VMEM = pl.BlockSpec(memory_space=pltpu.VMEM)
ANY = pl.BlockSpec(memory_space=pl.ANY)


def mm(a, b):
    return jnp.dot(a, b, preferred_element_type=F32)


def mm_nt(a, b):
    return lax.dot_general(a, b, (((1,), (1,)), ((), ())), preferred_element_type=F32)


def sigmoid(v):
    return 1.0 / (1.0 + jnp.exp(-v))


def peer(**coords):
    return dict(device_id=coords, device_id_type=MESH)


def gather_kernel(n, x_ref, bc_ref, k_ref, v_ref, xh, bch, bcn, ka, va,
                  ks, kr, vs, vr, hs, hr, loc):
    me = lax.axis_index("seq")
    rows = x_ref.shape[0]
    barrier = pltpu.get_barrier_semaphore()
    for off in range(1, n):
        pl.semaphore_signal(barrier, inc=1, **peer(seq=lax.rem(me + off, n)))
    pl.semaphore_wait(barrier, n - 1)

    def halo(slot, src, dst, to):
        return pltpu.make_async_remote_copy(
            src_ref=src, dst_ref=dst, send_sem=hs.at[slot], recv_sem=hr.at[slot], **peer(seq=to))

    nxt = lax.rem(me + 1, n)
    prv = lax.rem(me + n - 1, n)
    last = pl.ds(rows - EDGE, EDGE)
    cx = halo(0, x_ref.at[last], xh, nxt)
    cb = halo(1, bc_ref.at[last], bch, nxt)
    cn = halo(2, bc_ref.at[pl.ds(0, EDGE)], bcn, prv)

    @pl.when(me < n - 1)
    def _():
        cx.start()
        cb.start()

    @pl.when(me > 0)
    def _():
        cn.start()

    lk = pltpu.make_async_copy(k_ref, ka.at[me], loc.at[0])
    lv = pltpu.make_async_copy(v_ref, va.at[me], loc.at[1])
    lk.start()
    lv.start()

    def pair(off, to):
        return (
            pltpu.make_async_remote_copy(
                src_ref=k_ref, dst_ref=ka.at[me], send_sem=ks.at[off], recv_sem=kr.at[off],
                **peer(seq=to)),
            pltpu.make_async_remote_copy(
                src_ref=v_ref, dst_ref=va.at[me], send_sem=vs.at[off], recv_sem=vr.at[off],
                **peer(seq=to)),
        )

    for off in range(1, n):
        @pl.when(me + off < n)
        def _():
            a, b = pair(off, lax.rem(me + off, n))
            a.start()
            b.start()

    for off in range(1, n):
        @pl.when(me + off < n)
        def _():
            slot = lax.rem(me + off, n)
            ka[slot] = jnp.zeros(ka.shape[1:], ka.dtype)
            va[slot] = jnp.zeros(va.shape[1:], va.dtype)

    @pl.when(me == 0)
    def _():
        xh[...] = jnp.zeros(xh.shape, xh.dtype)
        bch[...] = jnp.zeros(bch.shape, bch.dtype)

    @pl.when(me == n - 1)
    def _():
        bcn[...] = jnp.zeros(bcn.shape, bcn.dtype)

    @pl.when(me < n - 1)
    def _():
        cx.wait_send()
        cb.wait_send()
        cn.wait_recv()

    @pl.when(me > 0)
    def _():
        cn.wait_send()
        cx.wait_recv()
        cb.wait_recv()

    lk.wait()
    lv.wait()
    for off in range(1, n):
        @pl.when(me + off < n)
        def _():
            a, b = pair(off, lax.rem(me + off, n))
            a.wait_send()
            b.wait_send()

        @pl.when(me - off >= 0)
        def _():
            a, b = pair(off, prv)
            a.wait_recv()
            b.wait_recv()


def gather(n, x_in, bc, keys, values):
    rows, width = keys.shape
    dma = pltpu.SemaphoreType.DMA
    return pl.pallas_call(
        functools.partial(gather_kernel, n),
        out_shape=(
            jax.ShapeDtypeStruct((EDGE, x_in.shape[1]), BF16),
            jax.ShapeDtypeStruct((EDGE, bc.shape[1]), BF16),
            jax.ShapeDtypeStruct((EDGE, bc.shape[1]), BF16),
            jax.ShapeDtypeStruct((n, rows, width), BF16),
            jax.ShapeDtypeStruct((n, rows, width), BF16),
        ),
        in_specs=[ANY] * 4,
        out_specs=(VMEM,) * 5,
        scratch_shapes=[dma((n,)), dma((n,)), dma((n,)), dma((n,)), dma((3,)), dma((3,)), dma((2,))],
        compiler_params=pltpu.CompilerParams(
            collective_id=0, has_side_effects=True, vmem_limit_bytes=40 * 2**20),
        name="gather",
    )(x_in, bc, keys, values)


def conv(x, halo, taps):
    width = taps.shape[0]
    rows = x.shape[0]
    full = jnp.concatenate([halo[EDGE - 8:], x], axis=0)
    total = None
    for tap in range(width):
        start = 8 - (width - 1) + tap
        term = taps[tap:tap + 1] * full[start:start + rows]
        total = term if total is None else total + term
    return total


def columns(row):
    return jnp.transpose(jnp.broadcast_to(row, (D, row.shape[1])))


def own_kernel(x_ref, xh_ref, w_ref, bc_ref, bch_ref, wbc_ref, run_ref, dm_ref,
               bcv_ref, of_ref, ob_ref, bt, ct):
    @pl.when(pl.program_id(0) == 0)
    def _():
        pre = conv(bc_ref[...].astype(F32), bch_ref[...].astype(F32), wbc_ref[...].astype(F32))
        act = pre * sigmoid(pre)
        bcv_ref[...] = act.astype(BF16)
        act = act.astype(BF16).astype(F32)
        bt[...] = jnp.transpose(act[:, :D]).astype(BF16)
        ct[...] = jnp.transpose(act[:, D:]).astype(BF16)

    pre = conv(x_ref[...].astype(F32), xh_ref[...].astype(F32), w_ref[...].astype(F32))
    xc = (pre * sigmoid(pre)).astype(BF16).astype(F32)
    row = run_ref[0]
    col = columns(row)
    final = row[:, row.shape[1] - 1:]
    of_ref[0] = mm(bt[...], (xc * jnp.exp(final - col)).astype(BF16))
    ob_ref[0] = mm(ct[...], (dm_ref[...].astype(F32) * jnp.exp(col)).astype(BF16))


def own_states(x_in, xh, conv_x, bc, bch, conv_bc, run_rows, d_mixed):
    rows, wide = x_in.shape
    heads = wide // D
    by_head = lambda r: pl.BlockSpec((r, D), lambda h: (0, h))
    whole = lambda a: pl.BlockSpec(a.shape, lambda h: (0,) * a.ndim)
    cube = pl.BlockSpec((1, D, D), lambda h: (h, 0, 0))
    return pl.pallas_call(
        own_kernel,
        grid=(heads,),
        out_shape=(
            jax.ShapeDtypeStruct(bc.shape, BF16),
            jax.ShapeDtypeStruct((heads, D, D), F32),
            jax.ShapeDtypeStruct((heads, D, D), F32),
        ),
        in_specs=[by_head(rows), by_head(EDGE), by_head(conv_x.shape[0]), whole(bc), whole(bch),
                  whole(conv_bc), pl.BlockSpec((1, 1, rows), lambda h: (h, 0, 0)), by_head(rows)],
        out_specs=(whole(bc), cube, cube),
        scratch_shapes=[pltpu.VMEM((D, rows), BF16), pltpu.VMEM((D, rows), BF16)],
        name="own_states",
    )(x_in, xh, conv_x, bc, bch, conv_bc, run_rows, d_mixed)


def chain_kernel(n, size, of, ob, dec, s_in, g_in, sf, sb, fs, fr, bs, br):
    me = lax.axis_index("seq")
    chunks = of.shape[0] // size
    nxt = lax.rem(me + 1, n)
    prv = lax.rem(me + n - 1, n)
    barrier = pltpu.get_barrier_semaphore()
    for to in (nxt, prv):
        pl.semaphore_signal(barrier, inc=1, **peer(seq=to))
    pl.semaphore_wait(barrier, 2)

    def copy(stage, landing, send, recv, c, to):
        part = pl.ds(c * size, size)
        return pltpu.make_async_remote_copy(
            src_ref=stage.at[part], dst_ref=landing.at[part], send_sem=send.at[c],
            recv_sem=recv.at[c], **peer(seq=to))

    def hop(c, own, landing, stage, send, recv, to, first, last):
        part = pl.ds(c * size, size)

        @pl.when(first)
        def _():
            landing[part] = jnp.zeros((size,) + landing.shape[1:], landing.dtype)
            stage[part] = own[part].astype(BF16)

        @pl.when(jnp.logical_not(first))
        def _():
            copy(stage, landing, send, recv, c, to).wait_recv()

            @pl.when(jnp.logical_not(last))
            def _():
                stage[part] = (dec[part] * landing[part].astype(F32) + own[part]).astype(BF16)

        @pl.when(jnp.logical_not(last))
        def _():
            copy(stage, landing, send, recv, c, to).start()

    def step(t, carry):
        f = t - me
        b = t - (n - 1 - me)

        @pl.when(jnp.logical_and(f >= 0, f < chunks))
        def _():
            hop(f, of, s_in, sf, fs, fr, nxt, me == 0, me == n - 1)

        @pl.when(jnp.logical_and(b >= 0, b < chunks))
        def _():
            hop(b, ob, g_in, sb, bs, br, prv, me == n - 1, me == 0)

        return carry

    lax.fori_loop(0, n - 1 + chunks, step, 0)

    def drain(c, carry):
        @pl.when(me < n - 1)
        def _():
            copy(sf, s_in, fs, fr, c, nxt).wait_send()

        @pl.when(me > 0)
        def _():
            copy(sb, g_in, bs, br, c, prv).wait_send()

        return carry

    lax.fori_loop(0, chunks, drain, 0)


def chain(n, of, ob, dec):
    heads = of.shape[0]
    size = 2 if heads % 2 == 0 else 1
    chunks = heads // size
    dma = pltpu.SemaphoreType.DMA
    out = jax.ShapeDtypeStruct(of.shape, BF16)
    return pl.pallas_call(
        functools.partial(chain_kernel, n, size),
        out_shape=(out, out),
        in_specs=[VMEM] * 3,
        out_specs=(VMEM, VMEM),
        scratch_shapes=[pltpu.VMEM(of.shape, BF16), pltpu.VMEM(of.shape, BF16),
                        dma((chunks,)), dma((chunks,)), dma((chunks,)), dma((chunks,))],
        compiler_params=pltpu.CompilerParams(
            collective_id=1, has_side_effects=True, vmem_limit_bytes=40 * 2**20),
        name="chain",
    )(of, ob, dec)


def main_kernel(ratio, heads, pos_ref, x_ref, xh_ref, w_ref, dm_ref, q_ref, bcv_ref, run_ref,
                skip_ref, k_ref, v_ref, s_ref, g_ref,
                mixed_ref, dq_ref, dk_ref, dv_ref, dx_ref, gh_ref, dla_ref, dbc_ref,
                kt, vt, inner, dinner, dka, dva, dbc):
    h = pl.program_id(0)
    rows = x_ref.shape[0]
    scale = D ** (-0.5)
    b = bcv_ref[:, :D]
    c = bcv_ref[:, D:]

    @pl.when(h == 0)
    def _():
        inner[...] = mm_nt(c, b)
        dinner[...] = jnp.zeros_like(dinner)
        dbc[...] = jnp.zeros_like(dbc)

    @pl.when(lax.rem(h, ratio) == 0)
    def _():
        kt[...] = jnp.transpose(k_ref[...].astype(F32)).astype(BF16)
        vt[...] = jnp.transpose(v_ref[...].astype(F32)).astype(BF16)
        dka[...] = jnp.zeros_like(dka)
        dva[...] = jnp.zeros_like(dva)

    dm = dm_ref[...]
    dmf = dm.astype(F32)
    q = q_ref[...]
    s = mm_nt(k_ref[...], q)
    upos = lax.broadcasted_iota(jnp.int32, s.shape, 0)
    tpos = lax.broadcasted_iota(jnp.int32, s.shape, 1) + pos_ref[0]
    s = jnp.where(upos <= tpos, s * (scale * math.log2(math.e)), -1e30)
    e = jnp.exp2(s - jnp.max(s, axis=0, keepdims=True))
    p = e * (1.0 / jnp.sum(e, axis=0, keepdims=True))
    pb = p.astype(BF16)
    att_t = mm(vt[...], pb)
    delta = jnp.sum(jnp.transpose(dmf) * att_t, axis=0, keepdims=True)
    ds = (p * (mm_nt(v_ref[...], dm) - delta)).astype(BF16)
    dq_ref[...] = jnp.transpose(mm(kt[...], ds)) * scale
    dka[...] += mm(ds, q)
    dva[...] += mm(pb, dm)

    @pl.when(lax.rem(h, ratio) == ratio - 1)
    def _():
        dk_ref[...] = (dka[...] * scale).astype(BF16)
        dv_ref[...] = dva[...].astype(BF16)

    w = w_ref[...].astype(F32)
    pre = conv(x_ref[...].astype(F32), xh_ref[...].astype(F32), w)
    sig = sigmoid(pre)
    xb = (pre * sig).astype(BF16)
    xf = xb.astype(F32)
    row = run_ref[0]
    col = columns(row)
    final = row[:, rows - 1:]
    t_i = lax.broadcasted_iota(jnp.int32, (rows, rows), 0)
    s_i = lax.broadcasted_iota(jnp.int32, (rows, rows), 1)
    fade = jnp.exp(jnp.where(t_i >= s_i, col - row, -1e30))
    mix = inner[...] * fade
    skip = skip_ref[0]
    enter = jnp.exp(col)
    tail = jnp.exp(final - col)
    state = s_ref[0]
    grad = g_ref[0]
    carried = enter * mm(c, state)
    y = mm(mix.astype(BF16), xb) + carried + skip * xf
    mixed_ref[...] = (y + jnp.transpose(att_t)).astype(BF16)
    back = tail * mm(b, grad)
    gx = mm(jnp.transpose(mix).astype(BF16), dm) + back + skip * dmf
    dmix = mm_nt(dm, xb)
    dinner[...] += dmix * fade
    dbc[:, D:] += mm_nt((enter * dmf).astype(BF16), state)
    dbc[:, :D] += mm_nt((tail * xf).astype(BF16), grad)
    dgap = dmix * mix
    away = xf * back
    net = dgap - jnp.transpose(dgap) + dmf * carried - away
    net = jnp.sum(net, axis=1, keepdims=True)
    dfinal = jnp.sum(away) + jnp.sum(
        jnp.exp(final) * jnp.sum(state.astype(F32) * grad.astype(F32), axis=0, keepdims=True))
    dla_ref[0] = jnp.sum(jnp.where(t_i >= s_i, net, 0.0), axis=0, keepdims=True) + dfinal

    g = gx * (sig * (1.0 + pre * (1.0 - sig)))
    gh_ref[...] = g[:EDGE].astype(BF16)
    width = w.shape[0]
    padded = jnp.concatenate([g, jnp.zeros((8, D), F32)], axis=0)
    total = None
    for tap in range(width):
        offset = width - 1 - tap
        term = w[tap:tap + 1] * padded[offset:offset + rows]
        total = term if total is None else total + term
    dx_ref[...] = total

    @pl.when(h == heads - 1)
    def _():
        di = dinner[...]
        dbc_ref[:, D:] = (dbc[:, D:] + mm(di.astype(BF16), b)).astype(BF16)
        dbc_ref[:, :D] = (dbc[:, :D] + mm(jnp.transpose(di).astype(BF16), c)).astype(BF16)


def main_part(pos, x_in, xh, conv_x, d_mixed, queries, bcv, run_rows, skip_rows, ka, va, s_in, g_in):
    rows, wide = x_in.shape
    heads = wide // D
    length, kv_wide = ka.shape
    ratio = heads // (kv_wide // D)
    by_head = lambda r: pl.BlockSpec((r, D), lambda h: (0, h))
    whole = lambda a: pl.BlockSpec(a.shape, lambda h: (0,) * a.ndim)
    cube = pl.BlockSpec((1, D, D), lambda h: (h, 0, 0))
    line = lambda r: pl.BlockSpec((1, 1, r), lambda h: (h, 0, 0))
    by_kv = pl.BlockSpec((length, D), lambda h: (0, h // ratio))
    shape = jax.ShapeDtypeStruct
    return pl.pallas_call(
        functools.partial(main_kernel, ratio, heads),
        grid=(heads,),
        out_shape=(
            shape((rows, wide), BF16), shape((rows, wide), F32), shape((length, kv_wide), BF16),
            shape((length, kv_wide), BF16), shape((rows, wide), F32), shape((EDGE, wide), BF16),
            shape((heads, 1, rows), F32), shape(bcv.shape, BF16),
        ),
        in_specs=[pl.BlockSpec(memory_space=pltpu.SMEM), by_head(rows), by_head(EDGE),
                  by_head(conv_x.shape[0]), by_head(rows), by_head(rows), whole(bcv), line(rows),
                  line(D), by_kv, by_kv, cube, cube],
        out_specs=(by_head(rows), by_head(rows), by_kv, by_kv, by_head(rows), by_head(EDGE),
                   line(rows), whole(bcv)),
        scratch_shapes=[
            pltpu.VMEM((D, length), BF16), pltpu.VMEM((D, length), BF16),
            pltpu.VMEM((rows, rows), F32), pltpu.VMEM((rows, rows), F32),
            pltpu.VMEM((length, D), F32), pltpu.VMEM((length, D), F32),
            pltpu.VMEM(bcv.shape, F32),
        ],
        compiler_params=pltpu.CompilerParams(vmem_limit_bytes=48 * 2**20),
        name="heads",
    )(pos, x_in, xh, conv_x, d_mixed, queries, bcv, run_rows, skip_rows, ka, va, s_in, g_in)


def sums_kernel(n, m, dk_ref, dv_ref, bc_ref, gh_ref, dk_out, dv_out, bc_out, bcn_out, gn_out,
                kb, vb, bb, nb, ks, kr, vs, vr, bs, br, ns, nr, hs, hr):
    me = lax.axis_index("seq")
    my = lax.axis_index("head")
    nxt = lax.rem(me + 1, n)
    prv = lax.rem(me + n - 1, n)
    barrier = pltpu.get_barrier_semaphore()
    count = 0
    for off in range(1, n):
        pl.semaphore_signal(barrier, inc=1, **peer(seq=lax.rem(me + off, n), head=my))
        count += 1
    for off in range(1, m):
        other = lax.rem(my + off, m)
        for to in (me, nxt, prv):
            pl.semaphore_signal(barrier, inc=1, **peer(seq=to, head=other))
            count += 1
    pl.semaphore_wait(barrier, count)

    def remote(src, dst, send, recv, seq, head):
        return pltpu.make_async_remote_copy(
            src_ref=src, dst_ref=dst, send_sem=send, recv_sem=recv, **peer(seq=seq, head=head))

    def pair(off, to):
        to = lax.rem(to + n, n)
        return (remote(dk_ref.at[to], kb.at[off], ks.at[off], kr.at[off], to, my),
                remote(dv_ref.at[to], vb.at[off], vs.at[off], vr.at[off], to, my))

    def across(off):
        return remote(bc_ref, bb.at[off], bs.at[off], br.at[off], me, lax.rem(my + off, m))

    def before(off):
        return remote(bc_ref.at[pl.ds(0, EDGE)], nb.at[off], ns.at[off], nr.at[off], prv,
                      lax.rem(my + off, m))

    edge = remote(gh_ref, gn_out, hs, hr, prv, my)
    for off in range(1, n):
        @pl.when(me - off >= 0)
        def _():
            for cp in pair(off, me - off):
                cp.start()

    for off in range(1, m):
        across(off).start()

    @pl.when(me > 0)
    def _():
        edge.start()
        for off in range(m):
            before(off).start()

    total = bc_ref[...].astype(F32)
    for off in range(1, m):
        across(off).wait_recv()
        total += bb[off].astype(F32)
    bc_out[...] = total

    @pl.when(me < n - 1)
    def _():
        edge.wait_recv()
        after = None
        for off in range(m):
            before(off).wait_recv()
            part = nb[off].astype(F32)
            after = part if after is None else after + part
        bcn_out[...] = after

    @pl.when(me == n - 1)
    def _():
        gn_out[...] = jnp.zeros(gn_out.shape, gn_out.dtype)
        bcn_out[...] = jnp.zeros(bcn_out.shape, bcn_out.dtype)

    dk_out[...] = dk_ref[me].astype(F32)
    dv_out[...] = dv_ref[me].astype(F32)
    for off in range(1, n):
        @pl.when(me + off < n)
        def _():
            a, b = pair(off, me + off)
            a.wait_recv()
            b.wait_recv()
            dk_out[...] += kb[off].astype(F32)
            dv_out[...] += vb[off].astype(F32)

    for off in range(1, n):
        @pl.when(me - off >= 0)
        def _():
            for cp in pair(off, me - off):
                cp.wait_send()
    for off in range(1, m):
        across(off).wait_send()

    @pl.when(me > 0)
    def _():
        edge.wait_send()
        for off in range(m):
            before(off).wait_send()


def sums(n, m, dk, dv, dbc, gh):
    rows, width = dk.shape[1:]
    dma = pltpu.SemaphoreType.DMA
    shape = jax.ShapeDtypeStruct
    return pl.pallas_call(
        functools.partial(sums_kernel, n, m),
        out_shape=(shape((rows, width), F32), shape((rows, width), F32), shape(dbc.shape, F32),
                   shape((EDGE, dbc.shape[1]), F32), shape(gh.shape, BF16)),
        in_specs=[VMEM] * 4,
        out_specs=(VMEM,) * 5,
        scratch_shapes=[
            pltpu.VMEM((n, rows, width), BF16), pltpu.VMEM((n, rows, width), BF16),
            pltpu.VMEM((m,) + dbc.shape, BF16), pltpu.VMEM((m, EDGE, dbc.shape[1]), BF16),
            dma((n,)), dma((n,)), dma((n,)), dma((n,)), dma((m,)), dma((m,)), dma((m,)), dma((m,)),
            dma, dma],
        compiler_params=pltpu.CompilerParams(
            collective_id=2, has_side_effects=True, vmem_limit_bytes=40 * 2**20),
        name="sums",
    )(dk, dv, dbc, gh)


def silu_slope(pre):
    s = jax.nn.sigmoid(pre)
    return s * (1.0 + pre * (1.0 - s))


def shards(n, m, x_in, bc_in, conv_x, conv_bc, log_decay, skip, queries, keys, values, d_mixed):
    rows = x_in.shape[0]
    heads = x_in.shape[1] // D
    taps = conv_x.shape[0]
    edge = taps - 1
    bc = bc_in.reshape(rows, 2 * D)
    wbc = conv_bc.reshape(taps, 2 * D)
    xh, bch, bcn, ka, va = gather(n, x_in, bc, keys, values)
    running = jnp.cumsum(log_decay, axis=0)
    run_rows = running.T.reshape(heads, 1, rows)
    dec = jnp.broadcast_to(jnp.exp(running[-1])[:, None, None], (heads, 1, D))
    skip_rows = jnp.broadcast_to(skip[:, None, None], (heads, 1, D))
    bcv, of, ob = own_states(x_in, xh, conv_x, bc, bch, wbc, run_rows, d_mixed)
    s_in, g_in = chain(n, of, ob, dec)
    pos = (lax.axis_index("seq") * rows).astype(jnp.int32).reshape(1)
    mixed, dq, dk, dv, dx, gh, dla, dbc = main_part(
        pos, x_in, xh, conv_x, d_mixed, queries, bcv, run_rows, skip_rows,
        ka.reshape(n * rows, -1), va.reshape(n * rows, -1), s_in, g_in)
    d_keys, d_values, bcs, bca, gn = sums(
        n, m, dk.reshape(n, rows, -1), dv.reshape(n, rows, -1), dbc, gh)
    wx = conv_x.astype(F32)
    gnf = jnp.concatenate([jnp.zeros((edge, gn.shape[1]), F32), gn[:edge].astype(F32)], axis=0)
    fix = sum(wx[j] * gnf[edge - j:2 * edge - j] for j in range(taps))
    d_x_in = dx.at[rows - edge:].add(fix)
    wb = wbc.astype(F32)
    full = jnp.concatenate([bch[EDGE - edge:], bc, bcn[:edge]], axis=0).astype(F32)
    pre = sum(wb[j] * full[j:j + rows + edge] for j in range(taps))
    g = jnp.concatenate([bcs, bca[:edge]], axis=0) * silu_slope(pre)
    d_bc = sum(wb[j] * g[edge - j:edge - j + rows] for j in range(taps))
    return (mixed, dq, d_keys, d_values, d_x_in, d_bc.reshape(rows, 2, D), dla.reshape(heads, rows).T)


def solution(mesh):
    n, m = mesh.shape["seq"], mesh.shape["head"]
    grid = P("seq", "head")
    part = P("seq", None, None)
    in_specs = (grid, part, P(None, "head"), P(), grid, P("head"), grid, grid, grid, grid)
    out_specs = (grid, grid, grid, grid, grid, part, grid)
    return jax.shard_map(functools.partial(shards, n, m), mesh=mesh, in_specs=in_specs,
                         out_specs=out_specs, check_vma=False)
```

time: 503 us -> 168 us (0.33)
  waiting for transfers between devices: 264 us -> 0 us
  Pallas kernels: 0 us -> 150 us
  blocking collectives: 84 us -> 0 us
  matrix products: 43 us -> 0 us
  other arithmetic: 39.3 us -> 1.86 us
  local copies, waits for them, and re-layouts: 44.8 us -> 13.9 us
  between operations: 14.4 us -> 0.88 us
  starting transfers between devices: 11.3 us -> 0 us
    all_gather x2 -> x0, waiting for transfers between devices: 151 us -> none  [carried_in(): pieces = jax.tree.map(lambda part: lax.all_gather(part, axis), value)]
    pallas_call x0 -> x5, Pallas kernels: none -> 150 us  [the longest x1 61.7 us: chain(): pl.pallas_call(functools.partial(chain_kernel, n, size), out_shape=(out,...]
    reduce_scatter x2 -> x0, waiting for transfers between devices: 110 us -> none  [the longest x1 66.4 us: shards(): lax.psum_scatter(value_terms, 'seq', scatter_dimension=0, tiled=True)]
    all_gather x3 -> x0, blocking collectives: 84 us -> none  [the longest x1 34.4 us: shards(): lax.all_gather(values, 'seq', axis=0, tiled=True)]
    dot_general x19 -> x0, matrix products: 43 us -> none  [the longest x3 10.1 us: span_step(): jnp.einsum('tsh,shp->thp', inner[:, :, None] * fading, x_blk, precision=h...]
    select_n x14 -> x0, other arithmetic: 20.4 us -> none  [lap(): jnp.where(position < mine, new, old)]
    ppermute x4 -> x0, starting transfers between devices: 11.1 us -> none  [from_behind(): return lax.ppermute(block, axis, route)]
    reshape x4 -> x1, local copies, waits for them, and re-layouts: 9.19 us -> 0.72 us  [shards(): d_bc.reshape(rows, 2, D)]
  transfers between devices with their start and end apart: 9 -> 0, of which waited for: 5 -> 0; matrix products, arithmetic and copies ran while one was open for 16% -> 0% of each run, Pallas kernels for 0% -> 0%
where the time goes in v1:
time: 168 us; the launch traced here: 167 us
  Pallas kernels  150 us (89%)
  local copies, waits for them, and re-layouts  13.9 us (8%)
  other arithmetic  1.86 us (1%)
    pallas_call x1, Pallas kernels, chain(): pl.pallas_call(functools.partial(chain_kernel, n, size), out_shape=(out,...  61.7 us
    pallas_call x1, Pallas kernels, main_part(): pl.pallas_call(functools.partial(main_kernel, ratio, heads), grid=(heads,...  29.3 us
    pallas_call x1, Pallas kernels, sums(): pl.pallas_call(functools.partial(sums_kernel, n, m), out_shape=(shape((ro...  25 us
    pallas_call x1, Pallas kernels, gather(): pl.pallas_call(functools.partial(gather_kernel, n), out_shape=(jax.ShapeD...  23.3 us
    pallas_call x1, Pallas kernels, own_states(): pl.pallas_call(own_kernel, grid=(heads,), out_shape=(jax.ShapeDtypeStruct...  10.8 us
    unnamed x46, local copies, waits for them, and re-layouts  10.2 us

profile of v1, /device:TPU:0, one launch (start us, length us, event | category | flops | bytes accessed | tf_op | source)
XLA Modules:
  0.0 166.9 jit_solution(11336527240613193227)
XLA Ops:
  0.6 0.0 copy-start.15
  0.6 0.0 copy-start.16
  0.7 0.9 copy.25
  1.5 0.0 copy-start.5
  1.6 0.0 copy-done.15
  1.6 0.0 copy-done.16
  1.6 0.0 copy-start
  1.6 1.0 copy-done
  2.6 23.3 %gather.1 = (bf16[16,2048]{1,0:T(8,128)(2,1)S(1)}, bf16[16,256]{1,0:T(8,128)(2,1)S(1)}, bf16[16,256]{1,0:T(8,128)(2,1)S(1)}, bf16[8,128,256]{2,1,0:T(8,128)(2,1)S(1)}, bf16[8,128,256]{2,1,0:T(8,128)(2,1)S(1)}) custom-call(bf16[128,2048]{1,0:T(8,128)(2,1)S(1)} %copy-done, bf16[128,256]{1,0:T(8,128)(2,1)S(1)} %bitcast.30, bf16[128,256]{1,0:T(8,128)(2,1)S(1)} %copy-done.15, ...), custom_call_target="tpu_custom_call" | custom-call | tf_op jit(solution)/shard_map/gather/pallas_call | solution.py:134
  26.0 0.0 copy-done.5
  26.0 0.0 copy-start.11
  26.0 0.6 copy-done.11
  26.6 0.6 copy-done.17
  27.2 0.0 copy-done.18
  27.2 0.1 copy.17
  27.3 0.2 reduce_window_sum.11
  27.5 0.7 copy.18
  28.2 0.7 copy-done.19
  28.8 0.6 fusion.13
  29.4 10.8 %own_states.1 = (bf16[128,256]{1,0:T(8,128)(2,1)}, f32[16,128,128]{2,1,0:T(8,128)}, f32[16,128,128]{2,1,0:T(8,128)}) custom-call(bf16[128,2048]{1,0:T(8,128)(2,1)} %x_ref.5, bf16[16,2048]{1,0:T(8,128)(2,1)} %copy-done.11, bf16[4,2048]{1,0:T(4,128)(2,1)} %w_ref.3, bf16[128,256]{1,0:T(8,128)(2,1)} %bitcast.31, bf16[16,256]{1,0:T(8,128)(2,1)} %copy-done.17, ...), custom_call_target="tpu_custom_call" | custom-call | tf_op jit(solution)/shard_map/own_states/pallas_call | solution.py:194
  40.2 0.1 broadcast_in_dim.7.dec
  40.3 0.0 copy-start.3
  40.3 1.2 copy-done.3
  41.5 1.2 copy-done.4
  42.8 0.0 copy-start.12
  42.8 0.0 copy-start.14
  42.8 61.7 %chain.1 = (bf16[16,128,128]{2,1,0:T(8,128)(2,1)S(1)}, bf16[16,128,128]{2,1,0:T(8,128)(2,1)S(1)}) custom-call(f32[16,128,128]{2,1,0:T(8,128)S(1)} %copy-done.3, f32[16,128,128]{2,1,0:T(8,128)S(1)} %copy-done.4, f32[16,1,128]{2,1,0:T(1,128)S(1)} %broadcast_in_dim.7.dec), custom_call_target="tpu_custom_call" | custom-call | tf_op jit(solution)/shard_map/chain/pallas_call | solution.py:282
  104.5 0.0 copy-start.8
  104.5 0.8 copy-done.8
  105.3 0.0 copy-done.20
  105.3 0.1 broadcast_in_dim.6.skip_ref
  105.4 0.0 copy-done.1
  105.4 0.0 copy-done.2
  105.4 0.0 copy-done.7
  105.4 0.0 copy-done.12
  105.4 0.0 copy-done.14
  105.4 0.6 copy-done.10
  106.0 1.0 copy-done.9
  107.1 29.3 %heads.1 = (bf16[128,2048]{1,0:T(8,128)(2,1)}, f32[128,2048]{1,0:T(8,128)}, bf16[1024,256]{1,0:T(8,128)(2,1)S(1)}, bf16[1024,256]{1,0:T(8,128)(2,1)S(1)}, f32[12...) custom-call(s32[1]{0:T(128)} %bitcast.pos_ref, ...), custom_call_target="tpu_custom_call" | custom-call | tf_op jit(solution)/shard_map/heads/pallas_call | solution.py:403
  136.4 25.0 %sums.1 = (f32[128,256]{1,0:T(8,128)S(1)}, f32[128,256]{1,0:T(8,128)S(1)}, f32[128,256]{1,0:T(8,128)S(1)}, f32[16,256]{1,0:T(8,128)S(1)}, bf16[16,2048]{1,0:T(8,128)(2,1)S(1)}) custom-call(bf16[8,128,256]{2,1,0:T(8,128)(2,1)S(1)} %bitcast.33, bf16[8,128,256]{2,1,0:T(8,128)(2,1)S(1)} %bitcast.34, bf16[128,256]{1,0:T(8,128)(2,1)S(1)} %get-tuple-element.55.bc_ref, ...), custom_call_target="tpu_custom_call" | custom-call | tf_op jit(solution)/shard_map/sums/pallas_call | solution.py:528
  161.5 0.7 slice.103
  162.2 0.1 maximum_multiply_fusion
  162.3 0.1 fusion.3
  162.4 0.7 reshape.91
  163.2 0.9 fusion.10
  164.0 1.5 scatter-add.4
  165.6 0.7 copy.29
  166.2 0.7 copy.30
  (23 shorter events, 0.1 us)
Async XLA Ops:
  0.6 0.9 copy-start.15
  0.6 0.9 copy-start.16
  1.5 24.4 %copy-start.5 = (bf16[16,8,2,128]{3,1,2,0:T(8,128)(2,1)}, bf16[16,8,2,128]{3,1,2,0:T(8,128)(2,1)S(1)}, u32[]{:S(2)}) copy-start(bf16[16,8,2,128]{3,1,2,0:T(8,128)(2,1)S(1)} %copy.25) | copy-start | bytes 196612
  1.6 1.1 copy-start
  2.6 24.6 %copy-start.18 = (f32[128,16]{0,1:T(8,128)S(1)}, f32[128,16]{0,1:T(8,128)}, u32[]{:S(2)}) copy-start(f32[128,16]{0,1:T(8,128)} %param.16) | copy-start | bytes 24580
  26.0 0.6 copy-start.11
  26.6 0.6 copy-start.17
  28.2 0.7 copy-start.19
  40.3 1.2 copy-start.3
  41.5 1.2 copy-start.4
  42.7 62.6 %copy-start.20 = (f32[16]{0:T(128)S(1)}, f32[16]{0:T(128)}, u32[]{:S(2)}) copy-start(f32[16]{0:T(128)} %param.17) | copy-start | bytes 196
  42.7 62.6 %copy-start.1 = (bf16[128,2048]{1,0:T(8,128)(2,1)S(1)}, bf16[128,2048]{1,0:T(8,128)(2,1)}, u32[]{:S(2)}) copy-start(bf16[128,2048]{1,0:T(8,128)(2,1)} %x_ref.5) | copy-start | bytes 1572868
  42.7 62.7 %copy-start.2 = (bf16[128,2048]{1,0:T(8,128)(2,1)S(1)}, bf16[128,2048]{1,0:T(8,128)(2,1)}, u32[]{:S(2)}) copy-start(bf16[128,2048]{1,0:T(8,128)(2,1)} %dm_ref.3) | copy-start | bytes 1572868
  42.7 62.7 %copy-start.7 = (bf16[128,2048]{1,0:T(8,128)(2,1)S(1)}, bf16[128,2048]{1,0:T(8,128)(2,1)}, u32[]{:S(2)}) copy-start(bf16[128,2048]{1,0:T(8,128)(2,1)} %q_ref.1) | copy-start | bytes 1572868
  42.8 62.7 %copy-start.12 = (bf16[16,2048]{1,0:T(8,128)(2,1)S(1)}, bf16[16,2048]{1,0:T(8,128)(2,1)}, u32[]{:S(2)}) copy-start(bf16[16,2048]{1,0:T(8,128)(2,1)} %copy-done.11) | copy-start | bytes 196612
  42.8 62.7 %copy-start.14 = (bf16[128,256]{1,0:T(8,128)(2,1)S(1)}, bf16[128,256]{1,0:T(8,128)(2,1)}, u32[]{:S(2)}) copy-start(bf16[128,256]{1,0:T(8,128)(2,1)} %get-tuple-element.44.bcv_ref) | copy-start | bytes 196612
  104.5 0.8 copy-start.8
  105.3 0.7 copy-start.10
  105.3 0.7 copy-start.13
  106.0 1.0 copy-start.9
  136.4 25.7 %copy-start.6 = (bf16[16,8,2,128]{3,1,2,0:T(8,128)(2,1)S(1)}, bf16[16,8,2,128]{3,1,2,0:T(8,128)(2,1)}, u32[]{:S(2)}) copy-start(bf16[16,8,2,128]{3,1,2,0:T(8,128)(2,1)} %copy-done.5) | copy-start | bytes 196612

commit v2 on v1

v2 whole, which is shorter than its diff:
```python
import functools
import math

import jax
import jax.numpy as jnp
from jax import lax
from jax.experimental import pallas as pl
from jax.experimental.pallas import tpu as pltpu
from jax.sharding import PartitionSpec as P

D = 128
EDGE = 16
F32 = jnp.float32
BF16 = jnp.bfloat16
MESH = pl.DeviceIdType.MESH
VMEM = pl.BlockSpec(memory_space=pltpu.VMEM)
ANY = pl.BlockSpec(memory_space=pl.ANY)


def mm(a, b):
    return jnp.dot(a, b, preferred_element_type=F32)


def mm_nt(a, b):
    return lax.dot_general(a, b, (((1,), (1,)), ((), ())), preferred_element_type=F32)


def sigmoid(v):
    return 1.0 / (1.0 + jnp.exp(-v))


def peer(**coords):
    return dict(device_id=coords, device_id_type=MESH)


def conv(x, halo, taps):
    width = taps.shape[0]
    rows = x.shape[0]
    full = jnp.concatenate([halo[EDGE - 8:], x], axis=0)
    total = None
    for tap in range(width):
        start = 8 - (width - 1) + tap
        term = taps[tap:tap + 1] * full[start:start + rows]
        total = term if total is None else total + term
    return total


def columns(row):
    return jnp.transpose(jnp.broadcast_to(row, (D, row.shape[1])))


def first_kernel(n, x_ref, bc_ref, k_ref, v_ref, w_ref, wbc_ref, run_ref, dm_ref,
                 xh, bch, bcn, kva, bcv_ref, of_ref, ob_ref, bt, ct, zs, zr, fs, fr, hs, hr):
    me = lax.axis_index("seq")
    odd = lax.rem(me, 2)
    mate = me + 1 - 2 * odd
    half = n // 2
    rows = x_ref.shape[0]
    width = k_ref.shape[1]
    heads = x_ref.shape[1] // D
    nxt = lax.rem(me + 1, n)
    prv = lax.rem(me + n - 1, n)
    barrier = pltpu.get_barrier_semaphore()
    for off in range(1, n):
        pl.semaphore_signal(barrier, inc=1, **peer(seq=lax.rem(me + off, n)))
    kva[me, :, :width] = k_ref[...]
    kva[me, :, width:] = v_ref[...]
    pl.semaphore_wait(barrier, n - 1)

    def halo(slot, src, dst, to):
        return pltpu.make_async_remote_copy(
            src_ref=src, dst_ref=dst, send_sem=hs.at[slot], recv_sem=hr.at[slot], **peer(seq=to))

    last = pl.ds(rows - EDGE, EDGE)
    cx = halo(0, x_ref.at[last], xh, nxt)
    cb = halo(1, bc_ref.at[last], bch, nxt)
    cn = halo(2, bc_ref.at[pl.ds(0, EDGE)], bcn, prv)

    @pl.when(me < n - 1)
    def _():
        cb.start()
        cx.start()

    @pl.when(me > 0)
    def _():
        cn.start()

    def block(src, to, send, recv):
        return pltpu.make_async_remote_copy(
            src_ref=kva.at[src], dst_ref=kva.at[src], send_sem=send, recv_sem=recv, **peer(seq=to))

    def direct(k):
        return block(me, lax.rem(me + 2 * k, n), zs.at[k], zr.at[k])

    def arrive(k):
        return block(lax.rem(me - 2 * k + n, n), lax.rem(me + 2 * k, n), zs.at[k], zr.at[k])

    def forward(k):
        return block(lax.rem(me - 2 * k + n, n), mate, fs.at[k], fr.at[k])

    def handed(k):
        return block(lax.rem(mate - 2 * k + n, n), mate, fs.at[k], fr.at[k])

    for k in range(1, half):
        @pl.when(me + 2 * k < n)
        def _():
            direct(k).start()

    @pl.when(odd == 0)
    def _():
        forward(0).start()

    for off in range(1, n):
        @pl.when(me + off < n)
        def _():
            kva[lax.rem(me + off, n)] = jnp.zeros(kva.shape[1:], kva.dtype)

    @pl.when(me == 0)
    def _():
        xh[...] = jnp.zeros(xh.shape, xh.dtype)
        bch[...] = jnp.zeros(bch.shape, bch.dtype)

    @pl.when(me == n - 1)
    def _():
        bcn[...] = jnp.zeros(bcn.shape, bcn.dtype)

    @pl.when(me > 0)
    def _():
        cb.wait_recv()
        cx.wait_recv()

    pre = conv(bc_ref[...].astype(F32), bch[...].astype(F32), wbc_ref[...].astype(F32))
    act = (pre * sigmoid(pre)).astype(BF16)
    bcv_ref[...] = act
    act = act.astype(F32)
    bt[...] = jnp.transpose(act[:, :D]).astype(BF16)
    ct[...] = jnp.transpose(act[:, D:]).astype(BF16)

    def head(h, carry):
        lanes = pl.ds(pl.multiple_of(h * D, D), D)
        pre = conv(x_ref[:, lanes].astype(F32), xh[:, lanes].astype(F32), w_ref[:, lanes].astype(F32))
        xc = (pre * sigmoid(pre)).astype(BF16).astype(F32)
        row = run_ref[h]
        col = columns(row)
        final = row[:, rows - 1:]
        of_ref[h] = mm(bt[...], (xc * jnp.exp(final - col)).astype(BF16))
        ob_ref[h] = mm(ct[...], (dm_ref[:, lanes].astype(F32) * jnp.exp(col)).astype(BF16))
        return carry

    done = 0
    for k in range(1, half):
        upto = heads * k // half
        lax.fori_loop(done, upto, head, 0)
        done = upto

        @pl.when(me - 2 * k >= 0)
        def _():
            arrive(k).wait_recv()
            forward(k).start()

    lax.fori_loop(done, heads, head, 0)

    @pl.when(me < n - 1)
    def _():
        cb.wait_send()
        cx.wait_send()
        cn.wait_recv()

    @pl.when(me > 0)
    def _():
        cn.wait_send()

    @pl.when(odd == 0)
    def _():
        forward(0).wait_send()

    @pl.when(odd == 1)
    def _():
        handed(0).wait_recv()

    for k in range(1, half):
        @pl.when(me + 2 * k < n)
        def _():
            direct(k).wait_send()

        @pl.when(me - 2 * k >= 0)
        def _():
            forward(k).wait_send()

        @pl.when(mate - 2 * k >= 0)
        def _():
            handed(k).wait_recv()


def first_part(n, x_in, bc, keys, values, conv_x, conv_bc, run_rows, d_mixed):
    rows, width = keys.shape
    heads = x_in.shape[1] // D
    dma = pltpu.SemaphoreType.DMA
    shape = jax.ShapeDtypeStruct
    return pl.pallas_call(
        functools.partial(first_kernel, n),
        out_shape=(
            shape((EDGE, x_in.shape[1]), BF16), shape((EDGE, bc.shape[1]), BF16),
            shape((EDGE, bc.shape[1]), BF16), shape((n, rows, 2 * width), BF16),
            shape(bc.shape, BF16), shape((heads, D, D), F32), shape((heads, D, D), F32),
        ),
        in_specs=[VMEM] * 8,
        out_specs=(VMEM,) * 7,
        scratch_shapes=[pltpu.VMEM((D, rows), BF16), pltpu.VMEM((D, rows), BF16),
                        dma((n // 2,)), dma((n // 2,)), dma((n // 2,)), dma((n // 2,)),
                        dma((3,)), dma((3,))],
        compiler_params=pltpu.CompilerParams(
            collective_id=0, has_side_effects=True, vmem_limit_bytes=40 * 2**20),
        name="first",
    )(x_in, bc, keys, values, conv_x, conv_bc, run_rows, d_mixed)


def chain_kernel(n, size, of, ob, dec, kva, q_ref, dm_ref,
                 s_in, g_in, att_ref, dq_ref, dk_out, dv_out,
                 sf, sb, kt, vt, dka, dva, part, land, fs, fr, bs, br, ps, pr):
    me = lax.axis_index("seq")
    chunks = of.shape[0] // size
    rows, wide = q_ref.shape
    heads = wide // D
    kv_heads = kva.shape[2] // (2 * D)
    ratio = heads // kv_heads
    length = n * rows
    nxt = lax.rem(me + 1, n)
    prv = lax.rem(me + n - 1, n)
    barrier = pltpu.get_barrier_semaphore()
    for off in range(1, n):
        pl.semaphore_signal(barrier, inc=1, **peer(seq=lax.rem(me + off, n)))
    pl.semaphore_wait(barrier, n - 1)

    def copy(stage, landing, send, recv, c, to):
        piece = pl.ds(c * size, size)
        return pltpu.make_async_remote_copy(
            src_ref=stage.at[piece], dst_ref=landing.at[piece], send_sem=send.at[c],
            recv_sem=recv.at[c], **peer(seq=to))

    def hop(c, own, landing, stage, send, recv, to, first, last):
        piece = pl.ds(c * size, size)

        @pl.when(first)
        def _():
            landing[piece] = jnp.zeros((size,) + landing.shape[1:], landing.dtype)
            stage[piece] = own[piece].astype(BF16)

        @pl.when(jnp.logical_not(first))
        def _():
            copy(stage, landing, send, recv, c, to).wait_recv()

            @pl.when(jnp.logical_not(last))
            def _():
                stage[piece] = (dec[piece] * landing[piece].astype(F32) + own[piece]).astype(BF16)

        @pl.when(jnp.logical_not(last))
        def _():
            copy(stage, landing, send, recv, c, to).start()

    def lend(kv, off, to):
        return pltpu.make_async_remote_copy(
            src_ref=part.at[kv, to], dst_ref=land.at[kv, off], send_sem=ps.at[kv, off],
            recv_sem=pr.at[kv, off], **peer(seq=to))

    scale = D ** (-0.5)
    upos = lax.broadcasted_iota(jnp.int32, (length, rows), 0)
    tpos = lax.broadcasted_iota(jnp.int32, (length, rows), 1)

    def attend(h):
        kv = h // ratio
        lanes = pl.ds(pl.multiple_of(h * D, D), D)
        k = kva[:, :, pl.ds(pl.multiple_of(kv * D, D), D)].reshape(length, D)
        v = kva[:, :, pl.ds(pl.multiple_of((kv_heads + kv) * D, D), D)].reshape(length, D)

        @pl.when(lax.rem(h, ratio) == 0)
        def _():
            kt[...] = jnp.transpose(k.astype(F32)).astype(BF16)
            vt[...] = jnp.transpose(v.astype(F32)).astype(BF16)
            dka[...] = jnp.zeros_like(dka)
            dva[...] = jnp.zeros_like(dva)

        q = q_ref[:, lanes]
        dm = dm_ref[:, lanes]
        s = mm_nt(k, q)
        s = jnp.where(upos <= tpos + me * rows, s * (scale * math.log2(math.e)), -1e30)
        e = jnp.exp2(s - jnp.max(s, axis=0, keepdims=True))
        p = e * (1.0 / jnp.sum(e, axis=0, keepdims=True))
        pb = p.astype(BF16)
        att_t = mm(vt[...], pb)
        att_ref[:, lanes] = jnp.transpose(att_t)
        delta = jnp.sum(jnp.transpose(dm.astype(F32)) * att_t, axis=0, keepdims=True)
        ds = (p * (mm_nt(v, dm) - delta)).astype(BF16)
        dq_ref[:, lanes] = jnp.transpose(mm(kt[...], ds)) * scale
        dka[...] += mm(ds, q)
        dva[...] += mm(pb, dm)

        @pl.when(lax.rem(h, ratio) == ratio - 1)
        def _():
            part[kv, :, :, :D] = (dka[...] * scale).astype(BF16).reshape(n, rows, D)
            part[kv, :, :, D:] = dva[...].astype(BF16).reshape(n, rows, D)
            for off in range(1, n):
                @pl.when(me - off >= 0)
                def _():
                    lend(kv, off, lax.rem(me - off + n, n)).start()

    def step(t, carry):
        f = t - me
        b = t - (n - 1 - me)

        @pl.when(jnp.logical_and(f >= 0, f < chunks))
        def _():
            hop(f, of, s_in, sf, fs, fr, nxt, me == 0, me == n - 1)

        @pl.when(jnp.logical_and(b >= 0, b < chunks))
        def _():
            hop(b, ob, g_in, sb, bs, br, prv, me == n - 1, me == 0)

        @pl.when(t < heads)
        def _():
            attend(t)

        return carry

    lax.fori_loop(0, max(n - 1 + chunks, heads), step, 0)

    def drain(c, carry):
        @pl.when(me < n - 1)
        def _():
            copy(sf, s_in, fs, fr, c, nxt).wait_send()

        @pl.when(me > 0)
        def _():
            copy(sb, g_in, bs, br, c, prv).wait_send()

        return carry

    lax.fori_loop(0, chunks, drain, 0)
    for kv in range(kv_heads):
        cols = slice(kv * D, kv * D + D)
        own = part[kv, me].astype(F32)
        dk_out[:, cols] = own[:, :D]
        dv_out[:, cols] = own[:, D:]
        for off in range(1, n):
            @pl.when(me + off < n)
            def _():
                lend(kv, off, prv).wait_recv()
                came = land[kv, off].astype(F32)
                dk_out[:, cols] += came[:, :D]
                dv_out[:, cols] += came[:, D:]

    for kv in range(kv_heads):
        for off in range(1, n):
            @pl.when(me - off >= 0)
            def _():
                lend(kv, off, lax.rem(me - off + n, n)).wait_send()


def chain(n, of, ob, dec, kva, queries, d_mixed):
    heads = of.shape[0]
    rows, wide = queries.shape
    width = kva.shape[2] // 2
    kv_heads = width // D
    size = 2 if heads % 2 == 0 else 1
    chunks = heads // size
    dma = pltpu.SemaphoreType.DMA
    shape = jax.ShapeDtypeStruct
    out = shape(of.shape, BF16)
    return pl.pallas_call(
        functools.partial(chain_kernel, n, size),
        out_shape=(out, out, shape((rows, wide), F32), shape((rows, wide), F32),
                   shape((rows, width), F32), shape((rows, width), F32)),
        in_specs=[VMEM] * 6,
        out_specs=(VMEM,) * 6,
        scratch_shapes=[
            pltpu.VMEM(of.shape, BF16), pltpu.VMEM(of.shape, BF16),
            pltpu.VMEM((D, n * rows), BF16), pltpu.VMEM((D, n * rows), BF16),
            pltpu.VMEM((n * rows, D), F32), pltpu.VMEM((n * rows, D), F32),
            pltpu.VMEM((kv_heads, n, rows, 2 * D), BF16), pltpu.VMEM((kv_heads, n, rows, 2 * D), BF16),
            dma((chunks,)), dma((chunks,)), dma((chunks,)), dma((chunks,)),
            dma((kv_heads, n)), dma((kv_heads, n))],
        compiler_params=pltpu.CompilerParams(
            collective_id=1, has_side_effects=True, vmem_limit_bytes=48 * 2**20),
        name="chain",
    )(of, ob, dec, kva, queries, d_mixed)


def ssd_kernel(heads, x_ref, xh_ref, w_ref, dm_ref, bcv_ref, run_ref, skip_ref, att_ref, s_ref, g_ref,
               mixed_ref, dx_ref, gh_ref, dla_ref, dbc_ref, inner, dinner, dbc):
    h = pl.program_id(0)
    rows = x_ref.shape[0]
    b = bcv_ref[:, :D]
    c = bcv_ref[:, D:]

    @pl.when(h == 0)
    def _():
        inner[...] = mm_nt(c, b)
        dinner[...] = jnp.zeros_like(dinner)
        dbc[...] = jnp.zeros_like(dbc)

    dm = dm_ref[...]
    dmf = dm.astype(F32)
    w = w_ref[...].astype(F32)
    pre = conv(x_ref[...].astype(F32), xh_ref[...].astype(F32), w)
    sig = sigmoid(pre)
    xb = (pre * sig).astype(BF16)
    xf = xb.astype(F32)
    row = run_ref[0]
    col = columns(row)
    final = row[:, rows - 1:]
    t_i = lax.broadcasted_iota(jnp.int32, (rows, rows), 0)
    s_i = lax.broadcasted_iota(jnp.int32, (rows, rows), 1)
    fade = jnp.exp(jnp.where(t_i >= s_i, col - row, -1e30))
    mix = inner[...] * fade
    skip = skip_ref[0]
    enter = jnp.exp(col)
    tail = jnp.exp(final - col)
    state = s_ref[0]
    grad = g_ref[0]
    carried = enter * mm(c, state)
    y = mm(mix.astype(BF16), xb) + carried + skip * xf
    mixed_ref[...] = (y + att_ref[...]).astype(BF16)
    back = tail * mm(b, grad)
    gx = mm(jnp.transpose(mix).astype(BF16), dm) + back + skip * dmf
    dmix = mm_nt(dm, xb)
    dinner[...] += dmix * fade
    dbc[:, D:] += mm_nt((enter * dmf).astype(BF16), state)
    dbc[:, :D] += mm_nt((tail * xf).astype(BF16), grad)
    dgap = dmix * mix
    away = xf * back
    net = dgap - jnp.transpose(dgap) + dmf * carried - away
    net = jnp.sum(net, axis=1, keepdims=True)
    dfinal = jnp.sum(away) + jnp.sum(
        jnp.exp(final) * jnp.sum(state.astype(F32) * grad.astype(F32), axis=0, keepdims=True))
    dla_ref[0] = jnp.sum(jnp.where(t_i >= s_i, net, 0.0), axis=0, keepdims=True) + dfinal

    g = gx * (sig * (1.0 + pre * (1.0 - sig)))
    gh_ref[...] = g[:EDGE].astype(BF16)
    width = w.shape[0]
    padded = jnp.concatenate([g, jnp.zeros((8, D), F32)], axis=0)
    total = None
    for tap in range(width):
        offset = width - 1 - tap
        term = w[tap:tap + 1] * padded[offset:offset + rows]
        total = term if total is None else total + term
    dx_ref[...] = total

    @pl.when(h == heads - 1)
    def _():
        di = dinner[...]
        dbc_ref[:, D:] = (dbc[:, D:] + mm(di.astype(BF16), b)).astype(BF16)
        dbc_ref[:, :D] = (dbc[:, :D] + mm(jnp.transpose(di).astype(BF16), c)).astype(BF16)


def ssd_part(x_in, xh, conv_x, d_mixed, bcv, run_rows, skip_rows, att, s_in, g_in):
    rows, wide = x_in.shape
    heads = wide // D
    by_head = lambda r: pl.BlockSpec((r, D), lambda h: (0, h))
    whole = lambda a: pl.BlockSpec(a.shape, lambda h: (0,) * a.ndim)
    cube = pl.BlockSpec((1, D, D), lambda h: (h, 0, 0))
    line = lambda r: pl.BlockSpec((1, 1, r), lambda h: (h, 0, 0))
    shape = jax.ShapeDtypeStruct
    return pl.pallas_call(
        functools.partial(ssd_kernel, heads),
        grid=(heads,),
        out_shape=(
            shape((rows, wide), BF16), shape((rows, wide), F32), shape((EDGE, wide), BF16),
            shape((heads, 1, rows), F32), shape(bcv.shape, BF16),
        ),
        in_specs=[by_head(rows), by_head(EDGE), by_head(conv_x.shape[0]), by_head(rows), whole(bcv),
                  line(rows), line(D), by_head(rows), cube, cube],
        out_specs=(by_head(rows), by_head(rows), by_head(EDGE), line(rows), whole(bcv)),
        scratch_shapes=[pltpu.VMEM((rows, rows), F32), pltpu.VMEM((rows, rows), F32),
                        pltpu.VMEM(bcv.shape, F32)],
        name="ssd",
    )(x_in, xh, conv_x, d_mixed, bcv, run_rows, skip_rows, att, s_in, g_in)


def sums_kernel(n, m, bc_ref, gh_ref, bc_out, bcn_out, gn_out, bb, nb, bs, br, ns, nr, hs, hr):
    me = lax.axis_index("seq")
    my = lax.axis_index("head")
    nxt = lax.rem(me + 1, n)
    prv = lax.rem(me + n - 1, n)
    barrier = pltpu.get_barrier_semaphore()
    count = 0
    for to in (nxt, prv):
        pl.semaphore_signal(barrier, inc=1, **peer(seq=to, head=my))
        count += 1
    for off in range(1, m):
        other = lax.rem(my + off, m)
        for to in (me, nxt, prv):
            pl.semaphore_signal(barrier, inc=1, **peer(seq=to, head=other))
            count += 1
    pl.semaphore_wait(barrier, count)

    def remote(src, dst, send, recv, seq, head):
        return pltpu.make_async_remote_copy(
            src_ref=src, dst_ref=dst, send_sem=send, recv_sem=recv, **peer(seq=seq, head=head))

    def across(off):
        return remote(bc_ref, bb.at[off], bs.at[off], br.at[off], me, lax.rem(my + off, m))

    def before(off):
        return remote(bc_ref.at[pl.ds(0, EDGE)], nb.at[off], ns.at[off], nr.at[off], prv,
                      lax.rem(my + off, m))

    edge = remote(gh_ref, gn_out, hs, hr, prv, my)
    for off in range(1, m):
        across(off).start()

    @pl.when(me > 0)
    def _():
        edge.start()
        for off in range(m):
            before(off).start()

    total = bc_ref[...].astype(F32)
    for off in range(1, m):
        across(off).wait_recv()
        total += bb[off].astype(F32)
    bc_out[...] = total

    @pl.when(me < n - 1)
    def _():
        edge.wait_recv()
        after = None
        for off in range(m):
            before(off).wait_recv()
            part = nb[off].astype(F32)
            after = part if after is None else after + part
        bcn_out[...] = after

    @pl.when(me == n - 1)
    def _():
        gn_out[...] = jnp.zeros(gn_out.shape, gn_out.dtype)
        bcn_out[...] = jnp.zeros(bcn_out.shape, bcn_out.dtype)

    for off in range(1, m):
        across(off).wait_send()

    @pl.when(me > 0)
    def _():
        edge.wait_send()
        for off in range(m):
            before(off).wait_send()


def sums(n, m, dbc, gh):
    dma = pltpu.SemaphoreType.DMA
    shape = jax.ShapeDtypeStruct
    return pl.pallas_call(
        functools.partial(sums_kernel, n, m),
        out_shape=(shape(dbc.shape, F32), shape((EDGE, dbc.shape[1]), F32), shape(gh.shape, BF16)),
        in_specs=[VMEM] * 2,
        out_specs=(VMEM,) * 3,
        scratch_shapes=[
            pltpu.VMEM((m,) + dbc.shape, BF16), pltpu.VMEM((m, EDGE, dbc.shape[1]), BF16),
            dma((m,)), dma((m,)), dma((m,)), dma((m,)), dma, dma],
        compiler_params=pltpu.CompilerParams(collective_id=2, has_side_effects=True),
        name="sums",
    )(dbc, gh)


def silu_slope(pre):
    s = jax.nn.sigmoid(pre)
    return s * (1.0 + pre * (1.0 - s))


def shards(n, m, x_in, bc_in, conv_x, conv_bc, log_decay, skip, queries, keys, values, d_mixed):
    rows = x_in.shape[0]
    heads = x_in.shape[1] // D
    taps = conv_x.shape[0]
    edge = taps - 1
    bc = bc_in.reshape(rows, 2 * D)
    wbc = conv_bc.reshape(taps, 2 * D)
    running = jnp.cumsum(log_decay, axis=0)
    run_rows = running.T.reshape(heads, 1, rows)
    dec = jnp.broadcast_to(jnp.exp(running[-1])[:, None, None], (heads, 1, D))
    skip_rows = jnp.broadcast_to(skip[:, None, None], (heads, 1, D))
    xh, bch, bcn, kva, bcv, of, ob = first_part(
        n, x_in, bc, keys, values, conv_x, wbc, run_rows, d_mixed)
    s_in, g_in, att, dq, d_keys, d_values = chain(n, of, ob, dec, kva, queries, d_mixed)
    mixed, dx, gh, dla, dbc = ssd_part(
        x_in, xh, conv_x, d_mixed, bcv, run_rows, skip_rows, att, s_in, g_in)
    bcs, bca, gn = sums(n, m, dbc, gh)
    wx = conv_x.astype(F32)
    gnf = jnp.concatenate([jnp.zeros((edge, gn.shape[1]), F32), gn[:edge].astype(F32)], axis=0)
    fix = sum(wx[j] * gnf[edge - j:2 * edge - j] for j in range(taps))
    d_x_in = dx.at[rows - edge:].add(fix)
    wb = wbc.astype(F32)
    full = jnp.concatenate([bch[EDGE - edge:], bc, bcn[:edge]], axis=0).astype(F32)
    pre = sum(wb[j] * full[j:j + rows + edge] for j in range(taps))
    g = jnp.concatenate([bcs, bca[:edge]], axis=0) * silu_slope(pre)
    d_bc = sum(wb[j] * g[edge - j:edge - j + rows] for j in range(taps))
    return (mixed, dq, d_keys, d_values, d_x_in, d_bc.reshape(rows, 2, D), dla.reshape(heads, rows).T)


def solution(mesh):
    n, m = mesh.shape["seq"], mesh.shape["head"]
    grid = P("seq", "head")
    part = P("seq", None, None)
    in_specs = (grid, part, P(None, "head"), P(), grid, P("head"), grid, grid, grid, grid)
    out_specs = (grid, grid, grid, grid, grid, part, grid)
    return jax.shard_map(functools.partial(shards, n, m), mesh=mesh, in_specs=in_specs,
                         out_specs=out_specs, check_vma=False)
```

time: 168 us -> 137 us (0.82)
  Pallas kernels: 150 us -> 116 us
  local copies, waits for them, and re-layouts: 13.9 us -> 17 us
    pallas_call x4 -> x3, Pallas kernels: 88.5 us -> 36.5 us  [the longest x1 14.6 us: first_part(): pl.pallas_call(functools.partial(first_kernel, n), out_shape=(shape((EDGE...]
    pallas_call x1, Pallas kernels: 61.7 us -> 79.7 us  [chain(): pl.pallas_call(functools.partial(chain_kernel, n, size), out_shape=(out,...]
    unnamed x46 -> x45, local copies, waits for them, and re-layouts: 10.2 us -> 13.2 us
where the time goes in v2:
time: 137 us; the launch traced here: 136 us
  Pallas kernels  116 us (85%)
  local copies, waits for them, and re-layouts  17 us (12%)
  other arithmetic  2.06 us (2%)
    pallas_call x1, Pallas kernels, chain(): pl.pallas_call(functools.partial(chain_kernel, n, size), out_shape=(out,...  79.7 us
    pallas_call x1, Pallas kernels, first_part(): pl.pallas_call(functools.partial(first_kernel, n), out_shape=(shape((EDGE...  14.6 us
    unnamed x45, local copies, waits for them, and re-layouts  13.2 us
    pallas_call x1, Pallas kernels, ssd_part(): pl.pallas_call(functools.partial(ssd_kernel, heads), grid=(heads,), out_s...  13.1 us
    pallas_call x1, Pallas kernels, sums(): pl.pallas_call(functools.partial(sums_kernel, n, m), out_shape=(shape(dbc...  8.75 us

profile of v2, /device:TPU:0, one launch (start us, length us, event | category | flops | bytes accessed | tf_op | source)
XLA Modules:
  0.0 136.1 jit_solution(153068205811780402)
XLA Ops:
  0.6 0.8 copy.17
  1.4 0.0 copy-start.17
  1.4 0.2 reduce_window_sum.11
  1.6 0.0 copy-start.13
  1.7 0.0 copy-start.11
  1.7 0.6 copy-done.17
  2.3 0.0 copy-start.9
  2.3 0.0 copy-start.12
  2.3 0.0 copy-start.18
  2.3 0.7 copy-done.18
  3.0 0.0 copy-done.11
  3.0 0.0 copy-done.13
  3.0 0.0 copy-done.9
  3.0 0.1 copy-done.12
  3.1 0.0 copy-start
  3.1 1.0 copy-done
  4.2 1.0 copy-done.2
  5.2 14.6 %first.1 = (bf16[16,2048]{1,0:T(8,128)(2,1)S(1)}, bf16[16,256]{1,0:T(8,128)(2,1)S(1)}, bf16[16,256]{1,0:T(8,128)(2,1)S(1)}, bf16[8,128,512]{2,1,0:T(8,128)(2,1)S...) custom-call(bf16[128,2048]{1,0:T(8,128)(2,1)S(1)} %copy-done.2, ...), custom_call_target="tpu_custom_call" | custom-call | tf_op jit(solution)/shard_map/first/pallas_call | solution.py:200
  19.9 0.0 copy-start.4
  19.9 1.0 copy-done.4
  20.8 1.0 copy-done.5
  21.8 0.6 copy-done.14
  22.4 0.6 copy-done.15
  23.1 0.1 broadcast_in_dim.7.dec
  23.1 0.0 copy-done.1
  23.2 0.0 copy-done.8
  23.2 79.7 %chain.1 = (bf16[16,128,128]{2,1,0:T(8,128)(2,1)S(1)}, bf16[16,128,128]{2,1,0:T(8,128)(2,1)S(1)}, f32[128,2048]{1,0:T(8,128)S(1)}, f32[128,2048]{1,0:T(8,128)S(1...) custom-call(f32[16,128,128]{2,1,0:T(8,128)S(1)} %get-tuple-element.42.of, f32[16,128,128]{2,1,0:T(8,128)} %copy-done.5, ...), custom_call_target="tpu_custom_call" | custom-call | tf_op jit(solution)/shard_map/chain/pallas_call | solution.py:369
  102.9 0.0 copy-start.3
  102.9 1.0 copy-done.3
  103.9 0.8 copy-done.6
  104.7 0.8 copy-done.7
  105.5 0.7 copy-done.19
  106.1 0.7 broadcast_in_dim.6.skip_ref
  106.8 13.1 %ssd.1 = (bf16[128,2048]{1,0:T(8,128)(2,1)}, f32[128,2048]{1,0:T(8,128)}, bf16[16,2048]{1,0:T(8,128)(2,1)}, f32[16,1,128]{2,1,0:T(1,128)}, bf16[128,256]{1,0:T(8,128)(2,1)}) custom-call(bf16[128,2048]{1,0:T(8,128)(2,1)} %x_ref.3, bf16[16,2048]{1,0:T(8,128)(2,1)} %copy-done.14, bf16[4,2048]{1,0:T(4,128)(2,1)} %w_ref.3, bf16[128,2048]{1,0:T(8,128)(2,1)} %dm_ref.5, ...), custom_call_target="tpu_custom_call" | custom-call | tf_op jit(solution)/shard_map/ssd/pallas_call | solution.py:463
  119.9 8.8 %sums.1 = (f32[128,256]{1,0:T(8,128)}, f32[16,256]{1,0:T(8,128)}, bf16[16,2048]{1,0:T(8,128)(2,1)}) custom-call(bf16[128,256]{1,0:T(8,128)(2,1)} %get-tuple-element.53.bc_ref, bf16[16,2048]{1,0:T(8,128)(2,1)} %get-tuple-element.54.gh_ref), custom_call_target="tpu_custom_call" | custom-call | tf_op jit(solution)/shard_map/sums/pallas_call | solution.py:551
  128.7 0.0 copy-start.16
  128.7 0.7 slice.102
  129.5 0.1 copy-done.16
  129.6 0.1 maximum_multiply_fusion
  129.7 0.1 fusion.3
  129.8 0.7 reshape.71
  130.5 0.8 slice_convert_fusion
  131.3 0.0 copy-done.10
  131.4 0.9 fusion.10
  132.3 1.5 %scatter-add.4 = f32[128,2048]{1,0:T(8,128)} dynamic-update-slice(f32[128,2048]{1,0:T(8,128)} %get-tuple-element.52, f32[3,2048]{1,0:T(4,128)S(1)} %fusion.10, s32[]{:T(128)} %constant.33.clone.1, s32[]{:T(128)} %constant.34.clone.1) | dynamic-update-slice | bytes 49156 | tf_op jit(solution)/shard_map/scatter-add | solution.py:589
  133.8 1.0 copy.30
  134.7 0.7 copy.31
  135.4 0.7 copy.32
  (21 shorter events, 0.2 us)
Async XLA Ops:
  1.4 0.8 copy-start.17
  1.6 1.4 %copy-start.13 = (bf16[128,256]{1,0:T(8,128)(2,1)S(1)}, bf16[128,256]{1,0:T(8,128)(2,1)}, u32[]{:S(2)}) copy-start(bf16[128,256]{1,0:T(8,128)(2,1)} %v_ref.1) | copy-start | bytes 196612
  1.7 1.4 copy-start.11
  2.3 0.7 copy-start.9
  2.3 0.9 copy-start.12
  2.3 0.7 copy-start.18
  3.1 1.0 copy-start
  4.2 1.0 copy-start.2
  5.2 17.9 %copy-start.1 = (bf16[128,2048]{1,0:T(8,128)(2,1)S(1)}, bf16[128,2048]{1,0:T(8,128)(2,1)}, u32[]{:S(2)}) copy-start(bf16[128,2048]{1,0:T(8,128)(2,1)} %dm_ref.5) | copy-start | bytes 1572868
  5.2 17.9 %copy-start.8 = (bf16[128,2048]{1,0:T(8,128)(2,1)S(1)}, bf16[128,2048]{1,0:T(8,128)(2,1)}, u32[]{:S(2)}) copy-start(bf16[128,2048]{1,0:T(8,128)(2,1)} %q_ref.1) | copy-start | bytes 1572868
  19.9 1.0 copy-start.4
  20.8 1.0 copy-start.5
  21.8 0.6 copy-start.14
  22.4 0.6 copy-start.15
  102.9 1.0 copy-start.3
  103.9 0.8 copy-start.6
  104.7 0.8 copy-start.7
  105.5 0.7 copy-start.19
  128.7 0.9 copy-start.16
  130.5 0.8 copy-start.10

commit v3 on v2

--- a/solution.py
+++ b/solution.py
@@ -49,8 +49,9 @@
     return jnp.transpose(jnp.broadcast_to(row, (D, row.shape[1])))
 
 
-def first_kernel(n, x_ref, bc_ref, k_ref, v_ref, w_ref, wbc_ref, run_ref, dm_ref,
-                 xh, bch, bcn, kva, bcv_ref, of_ref, ob_ref, bt, ct, zs, zr, fs, fr, hs, hr):
+def first_kernel(n, x_ref, bc_ref, k_ref, v_ref, w_ref, wbc_ref, run_ref, dm_ref, dec_ref,
+                 xh, bch, bcn, kva, bcv_ref, of_ref, ob_ref, rf_ref, rb_ref, rdec_ref,
+                 sf, sb, bt, ct, zs, zr, fs, fr, hs, hr, ofs, ofr, obs, obr, es, er):
     me = lax.axis_index("seq")
     odd = lax.rem(me, 2)
     mate = me + 1 - 2 * odd
@@ -85,6 +86,22 @@
     def _():
         cn.start()
 
+    share = heads // 2
+    swap = pltpu.make_async_remote_copy(
+        src_ref=dec_ref.at[pl.ds((1 - odd) * share, share)], dst_ref=rdec_ref, send_sem=es,
+        recv_sem=er, **peer(seq=mate))
+    swap.start()
+
+    def trade(i):
+        return (
+            pltpu.make_async_remote_copy(
+                src_ref=sf.at[i], dst_ref=rf_ref.at[i], send_sem=ofs.at[i], recv_sem=ofr.at[i],
+                **peer(seq=mate)),
+            pltpu.make_async_remote_copy(
+                src_ref=sb.at[i], dst_ref=rb_ref.at[i], send_sem=obs.at[i], recv_sem=obr.at[i],
+                **peer(seq=mate)),
+        )
+
     def block(src, to, send, recv):
         return pltpu.make_async_remote_copy(
             src_ref=kva.at[src], dst_ref=kva.at[src], send_sem=send, recv_sem=recv, **peer(seq=to))
@@ -136,15 +153,29 @@
     bt[...] = jnp.transpose(act[:, :D]).astype(BF16)
     ct[...] = jnp.transpose(act[:, D:]).astype(BF16)
 
-    def head(h, carry):
+    def head(i, carry):
+        h = lax.rem(i + (1 - odd) * share, heads)
         lanes = pl.ds(pl.multiple_of(h * D, D), D)
         pre = conv(x_ref[:, lanes].astype(F32), xh[:, lanes].astype(F32), w_ref[:, lanes].astype(F32))
         xc = (pre * sigmoid(pre)).astype(BF16).astype(F32)
         row = run_ref[h]
         col = columns(row)
         final = row[:, rows - 1:]
-        of_ref[h] = mm(bt[...], (xc * jnp.exp(final - col)).astype(BF16))
-        ob_ref[h] = mm(ct[...], (dm_ref[:, lanes].astype(F32) * jnp.exp(col)).astype(BF16))
+        own_f = mm(bt[...], (xc * jnp.exp(final - col)).astype(BF16))
+        own_b = mm(ct[...], (dm_ref[:, lanes].astype(F32) * jnp.exp(col)).astype(BF16))
+
+        @pl.when(i < share)
+        def _():
+            sf[i] = own_f.astype(BF16)
+            sb[i] = own_b.astype(BF16)
+            for cp in trade(i):
+                cp.start()
+
+        @pl.when(i >= share)
+        def _():
+            of_ref[i - share] = own_f
+            ob_ref[i - share] = own_b
+
         return carry
 
     done = 0
@@ -159,6 +190,14 @@
             forward(k).start()
 
     lax.fori_loop(done, heads, head, 0)
+    swap.wait()
+
+    def settle(i, carry):
+        for cp in trade(i):
+            cp.wait()
+        return carry
+
+    lax.fori_loop(0, share, settle, 0)
 
     @pl.when(me < n - 1)
     def _():
@@ -192,9 +231,9 @@
             handed(k).wait_recv()
 
 
-def first_part(n, x_in, bc, keys, values, conv_x, conv_bc, run_rows, d_mixed):
+def first_part(n, x_in, bc, keys, values, conv_x, conv_bc, run_rows, d_mixed, dec):
     rows, width = keys.shape
-    heads = x_in.shape[1] // D
+    share = x_in.shape[1] // D // 2
     dma = pltpu.SemaphoreType.DMA
     shape = jax.ShapeDtypeStruct
     return pl.pallas_call(
@@ -202,30 +241,41 @@
         out_shape=(
             shape((EDGE, x_in.shape[1]), BF16), shape((EDGE, bc.shape[1]), BF16),
             shape((EDGE, bc.shape[1]), BF16), shape((n, rows, 2 * width), BF16),
-            shape(bc.shape, BF16), shape((heads, D, D), F32), shape((heads, D, D), F32),
+            shape(bc.shape, BF16), shape((share, D, D), F32), shape((share, D, D), F32),
+            shape((share, D, D), BF16), shape((share, D, D), BF16), shape((share, 1, D), F32),
         ),
-        in_specs=[VMEM] * 8,
-        out_specs=(VMEM,) * 7,
-        scratch_shapes=[pltpu.VMEM((D, rows), BF16), pltpu.VMEM((D, rows), BF16),
+        in_specs=[VMEM] * 9,
+        out_specs=(VMEM,) * 10,
+        scratch_shapes=[pltpu.VMEM((share, D, D), BF16), pltpu.VMEM((share, D, D), BF16),
+                        pltpu.VMEM((D, rows), BF16), pltpu.VMEM((D, rows), BF16),
                         dma((n // 2,)), dma((n // 2,)), dma((n // 2,)), dma((n // 2,)),
-                        dma((3,)), dma((3,))],
+                        dma((3,)), dma((3,)), dma((share,)), dma((share,)), dma((share,)),
+                        dma((share,)), dma, dma],
         compiler_params=pltpu.CompilerParams(
-            collective_id=0, has_side_effects=True, vmem_limit_bytes=40 * 2**20),
+            collective_id=0, has_side_effects=True, vmem_limit_bytes=20 * 2**20),
         name="first",
-    )(x_in, bc, keys, values, conv_x, conv_bc, run_rows, d_mixed)
-
-
-def chain_kernel(n, size, of, ob, dec, kva, q_ref, dm_ref,
+    )(x_in, bc, keys, values, conv_x, conv_bc, run_rows, d_mixed, dec)
+
+
+def chain_kernel(n, size, of, ob, rf, rb, dec, rdec, kva, q_ref, dm_ref,
                  s_in, g_in, att_ref, dq_ref, dk_out, dv_out,
-                 sf, sb, kt, vt, dka, dva, part, land, fs, fr, bs, br, ps, pr):
+                 af, ab, sf, sb, mf, mb, kt, vt, dka, dva, part, land,
+                 fs, fr, bs, br, mfs, mfr, mbs, mbr, ps, pr):
     me = lax.axis_index("seq")
-    chunks = of.shape[0] // size
+    share = of.shape[0]
+    chunks = share // size
     rows, wide = q_ref.shape
     heads = wide // D
     kv_heads = kva.shape[2] // (2 * D)
     ratio = heads // kv_heads
     length = n * rows
-    nxt = lax.rem(me + 1, n)
+    odd = lax.rem(me, 2)
+    mate = me + 1 - 2 * odd
+    base = odd * share
+    level = me // 2
+    levels = n // 2
+    up = lax.rem(me + 2, n)
+    down = lax.rem(me + n - 2, n)
     prv = lax.rem(me + n - 1, n)
     barrier = pltpu.get_barrier_semaphore()
     for off in range(1, n):
@@ -238,25 +288,52 @@
             src_ref=stage.at[piece], dst_ref=landing.at[piece], send_sem=send.at[c],
             recv_sem=recv.at[c], **peer(seq=to))
 
-    def hop(c, own, landing, stage, send, recv, to, first, last):
+    def give(stage, out, send, recv, c, start):
+        return pltpu.make_async_remote_copy(
+            src_ref=stage.at[pl.ds(c * size, size)], dst_ref=out.at[pl.ds(start + c * size, size)],
+            send_sem=send.at[c], recv_sem=recv.at[c], **peer(seq=mate))
+
+    is_odd = odd == 1
+
+    def ahead(c, x):
         piece = pl.ds(c * size, size)
+        mine, other = of[piece], rf[piece].astype(F32)
+        even_f, odd_f = jnp.where(is_odd, other, mine), jnp.where(is_odd, mine, other)
+        even_d = jnp.where(is_odd, rdec[piece], dec[pl.ds(base + c * size, size)])
+        odd_d = jnp.where(is_odd, dec[pl.ds(base + c * size, size)], rdec[piece])
+        middle = even_d * x + even_f
+        return jnp.where(is_odd, middle, x), jnp.where(is_odd, x, middle), odd_d * middle + odd_f
+
+    def behind(c, x):
+        piece = pl.ds(c * size, size)
+        mine, other = ob[piece], rb[piece].astype(F32)
+        even_b, odd_b = jnp.where(is_odd, other, mine), jnp.where(is_odd, mine, other)
+        even_d = jnp.where(is_odd, rdec[piece], dec[pl.ds(base + c * size, size)])
+        odd_d = jnp.where(is_odd, dec[pl.ds(base + c * size, size)], rdec[piece])
+        middle = odd_d * x + odd_b
+        return jnp.where(is_odd, x, middle), jnp.where(is_odd, middle, x), even_d * middle + even_b
+
+    def hop(c, join, landing, stage, send, recv, to, first, last, out, gift, gsend, grecv):
+        piece = pl.ds(c * size, size)
 
         @pl.when(first)
         def _():
             landing[piece] = jnp.zeros((size,) + landing.shape[1:], landing.dtype)
-            stage[piece] = own[piece].astype(BF16)
 
         @pl.when(jnp.logical_not(first))
         def _():
             copy(stage, landing, send, recv, c, to).wait_recv()
 
-            @pl.when(jnp.logical_not(last))
-            def _():
-                stage[piece] = (dec[piece] * landing[piece].astype(F32) + own[piece]).astype(BF16)
+        mine, other, on = join(c, landing[piece].astype(F32))
+        stage[piece] = on.astype(BF16)
 
         @pl.when(jnp.logical_not(last))
         def _():
             copy(stage, landing, send, recv, c, to).start()
+
+        out[pl.ds(base + c * size, size)] = mine.astype(BF16)
+        gift[piece] = other.astype(BF16)
+        give(gift, out, gsend, grecv, c, base).start()
 
     def lend(kv, off, to):
         return pltpu.make_async_remote_copy(
@@ -305,16 +382,18 @@
                     lend(kv, off, lax.rem(me - off + n, n)).start()
 
     def step(t, carry):
-        f = t - me
-        b = t - (n - 1 - me)
+        f = t - level
+        b = t - (levels - 1 - level)
 
         @pl.when(jnp.logical_and(f >= 0, f < chunks))
         def _():
-            hop(f, of, s_in, sf, fs, fr, nxt, me == 0, me == n - 1)
+            hop(f, ahead, af, sf, fs, fr, up, level == 0, level == levels - 1,
+                s_in, mf, mfs, mfr)
 
         @pl.when(jnp.logical_and(b >= 0, b < chunks))
         def _():
-            hop(b, ob, g_in, sb, bs, br, prv, me == n - 1, me == 0)
+            hop(b, behind, ab, sb, bs, br, down, level == levels - 1, level == 0,
+                g_in, mb, mbs, mbr)
 
         @pl.when(t < heads)
         def _():
@@ -322,16 +401,21 @@
 
         return carry
 
-    lax.fori_loop(0, max(n - 1 + chunks, heads), step, 0)
+    lax.fori_loop(0, max(levels - 1 + chunks, heads), step, 0)
 
     def drain(c, carry):
-        @pl.when(me < n - 1)
-        def _():
-            copy(sf, s_in, fs, fr, c, nxt).wait_send()
-
-        @pl.when(me > 0)
-        def _():
-            copy(sb, g_in, bs, br, c, prv).wait_send()
+        @pl.when(level < levels - 1)
+        def _():
+            copy(sf, af, fs, fr, c, up).wait_send()
+
+        @pl.when(level > 0)
+        def _():
+            copy(sb, ab, bs, br, c, down).wait_send()
+
+        give(mf, s_in, mfs, mfr, c, base).wait_send()
+        give(mb, g_in, mbs, mbr, c, base).wait_send()
+        give(mf, s_in, mfs, mfr, c, share - base).wait_recv()
+        give(mb, g_in, mbs, mbr, c, share - base).wait_recv()
 
         return carry
 
@@ -356,37 +440,38 @@
                 lend(kv, off, lax.rem(me - off + n, n)).wait_send()
 
 
-def chain(n, of, ob, dec, kva, queries, d_mixed):
-    heads = of.shape[0]
+def chain(n, of, ob, rf, rb, dec, rdec, kva, queries, d_mixed):
+    share = of.shape[0]
     rows, wide = queries.shape
     width = kva.shape[2] // 2
     kv_heads = width // D
-    size = 2 if heads % 2 == 0 else 1
-    chunks = heads // size
+    size = 2 if share % 2 == 0 else 1
+    chunks = share // size
     dma = pltpu.SemaphoreType.DMA
     shape = jax.ShapeDtypeStruct
-    out = shape(of.shape, BF16)
+    out = shape((2 * share, D, D), BF16)
     return pl.pallas_call(
         functools.partial(chain_kernel, n, size),
         out_shape=(out, out, shape((rows, wide), F32), shape((rows, wide), F32),
                    shape((rows, width), F32), shape((rows, width), F32)),
-        in_specs=[VMEM] * 6,
+        in_specs=[VMEM] * 9,
         out_specs=(VMEM,) * 6,
         scratch_shapes=[
-            pltpu.VMEM(of.shape, BF16), pltpu.VMEM(of.shape, BF16),
+            *[pltpu.VMEM(of.shape, BF16) for _ in range(6)],
             pltpu.VMEM((D, n * rows), BF16), pltpu.VMEM((D, n * rows), BF16),
             pltpu.VMEM((n * rows, D), F32), pltpu.VMEM((n * rows, D), F32),
             pltpu.VMEM((kv_heads, n, rows, 2 * D), BF16), pltpu.VMEM((kv_heads, n, rows, 2 * D), BF16),
-            dma((chunks,)), dma((chunks,)), dma((chunks,)), dma((chunks,)),
+            *[dma((chunks,)) for _ in range(8)],
             dma((kv_heads, n)), dma((kv_heads, n))],
         compiler_params=pltpu.CompilerParams(
-            collective_id=1, has_side_effects=True, vmem_limit_bytes=48 * 2**20),
+            collective_id=1, has_side_effects=True, vmem_limit_bytes=28 * 2**20),
         name="chain",
-    )(of, ob, dec, kva, queries, d_mixed)
+    )(of, ob, rf, rb, dec, rdec, kva, queries, d_mixed)
 
 
 def ssd_kernel(heads, x_ref, xh_ref, w_ref, dm_ref, bcv_ref, run_ref, skip_ref, att_ref, s_ref, g_ref,
-               mixed_ref, dx_ref, gh_ref, dla_ref, dbc_ref, inner, dinner, dbc):
+               dqi_ref, dki_ref, dvi_ref, mixed_ref, dx_ref, gh_ref, dla_ref, dbc_ref,
+               dq_ref, dk_ref, dv_ref, inner, dinner, dbc):
     h = pl.program_id(0)
     rows = x_ref.shape[0]
     b = bcv_ref[:, :D]
@@ -398,6 +483,7 @@
         dinner[...] = jnp.zeros_like(dinner)
         dbc[...] = jnp.zeros_like(dbc)
 
+    dq_ref[...] = dqi_ref[...]
     dm = dm_ref[...]
     dmf = dm.astype(F32)
     w = w_ref[...].astype(F32)
@@ -447,12 +533,14 @@
 
     @pl.when(h == heads - 1)
     def _():
+        dk_ref[...] = dki_ref[...]
+        dv_ref[...] = dvi_ref[...]
         di = dinner[...]
         dbc_ref[:, D:] = (dbc[:, D:] + mm(di.astype(BF16), b)).astype(BF16)
         dbc_ref[:, :D] = (dbc[:, :D] + mm(jnp.transpose(di).astype(BF16), c)).astype(BF16)
 
 
-def ssd_part(x_in, xh, conv_x, d_mixed, bcv, run_rows, skip_rows, att, s_in, g_in):
+def ssd_part(x_in, xh, conv_x, d_mixed, bcv, run_rows, skip_rows, att, s_in, g_in, dq, dk, dv):
     rows, wide = x_in.shape
     heads = wide // D
     by_head = lambda r: pl.BlockSpec((r, D), lambda h: (0, h))
@@ -465,15 +553,18 @@
         grid=(heads,),
         out_shape=(
             shape((rows, wide), BF16), shape((rows, wide), F32), shape((EDGE, wide), BF16),
-            shape((heads, 1, rows), F32), shape(bcv.shape, BF16),
+            shape((heads, 1, rows), F32), shape(bcv.shape, BF16), shape((rows, wide), F32),
+            shape(dk.shape, F32), shape(dv.shape, F32),
         ),
         in_specs=[by_head(rows), by_head(EDGE), by_head(conv_x.shape[0]), by_head(rows), whole(bcv),
-                  line(rows), line(D), by_head(rows), cube, cube],
-        out_specs=(by_head(rows), by_head(rows), by_head(EDGE), line(rows), whole(bcv)),
+                  line(rows), line(D), by_head(rows), cube, cube, by_head(rows), whole(dk),
+                  whole(dv)],
+        out_specs=(by_head(rows), by_head(rows), by_head(EDGE), line(rows), whole(bcv),
+                   by_head(rows), whole(dk), whole(dv)),
         scratch_shapes=[pltpu.VMEM((rows, rows), F32), pltpu.VMEM((rows, rows), F32),
                         pltpu.VMEM(bcv.shape, F32)],
         name="ssd",
-    )(x_in, xh, conv_x, d_mixed, bcv, run_rows, skip_rows, att, s_in, g_in)
+    )(x_in, xh, conv_x, d_mixed, bcv, run_rows, skip_rows, att, s_in, g_in, dq, dk, dv)
 
 
 def sums_kernel(n, m, bc_ref, gh_ref, bc_out, bcn_out, gn_out, bb, nb, bs, br, ns, nr, hs, hr):
@@ -577,11 +668,11 @@
     run_rows = running.T.reshape(heads, 1, rows)
     dec = jnp.broadcast_to(jnp.exp(running[-1])[:, None, None], (heads, 1, D))
     skip_rows = jnp.broadcast_to(skip[:, None, None], (heads, 1, D))
-    xh, bch, bcn, kva, bcv, of, ob = first_part(
-        n, x_in, bc, keys, values, conv_x, wbc, run_rows, d_mixed)
-    s_in, g_in, att, dq, d_keys, d_values = chain(n, of, ob, dec, kva, queries, d_mixed)
-    mixed, dx, gh, dla, dbc = ssd_part(
-        x_in, xh, conv_x, d_mixed, bcv, run_rows, skip_rows, att, s_in, g_in)
+    xh, bch, bcn, kva, bcv, of, ob, rf, rb, rdec = first_part(
+        n, x_in, bc, keys, values, conv_x, wbc, run_rows, d_mixed, dec)
+    s_in, g_in, att, dq, dk, dv = chain(n, of, ob, rf, rb, dec, rdec, kva, queries, d_mixed)
+    mixed, dx, gh, dla, dbc, dq, d_keys, d_values = ssd_part(
+        x_in, xh, conv_x, d_mixed, bcv, run_rows, skip_rows, att, s_in, g_in, dq, dk, dv)
     bcs, bca, gn = sums(n, m, dbc, gh)
     wx = conv_x.astype(F32)
     gnf = jnp.concatenate([jnp.zeros((edge, gn.shape[1]), F32), gn[:edge].astype(F32)], axis=0)

time: 137 us -> 116 us (0.85)
  Pallas kernels: 116 us -> 96.7 us
  local copies, waits for them, and re-layouts: 17 us -> 15.1 us
    pallas_call x1, Pallas kernels: 79.7 us -> 51.6 us  [chain(): pl.pallas_call(functools.partial(chain_kernel, n, size), out_shape=(out,...]
    pallas_call x1, Pallas kernels: 14.6 us -> 22.5 us  [first_part(): pl.pallas_call(functools.partial(first_kernel, n), out_shape=(shape((EDGE...]
    unnamed x45 -> x44, local copies, waits for them, and re-layouts: 13.2 us -> 11.3 us
where the time goes in v3:
time: 116 us; the launch traced here: 115 us
  Pallas kernels  96.7 us (83%)
  local copies, waits for them, and re-layouts  15.1 us (13%)
  other arithmetic  2.06 us (2%)
    pallas_call x1, Pallas kernels, chain(): pl.pallas_call(functools.partial(chain_kernel, n, size), out_shape=(out,...  51.6 us
    pallas_call x1, Pallas kernels, first_part(): pl.pallas_call(functools.partial(first_kernel, n), out_shape=(shape((EDGE...  22.5 us
    pallas_call x1, Pallas kernels, ssd_part(): pl.pallas_call(functools.partial(ssd_kernel, heads), grid=(heads,), out_s...  13.9 us
    unnamed x44, local copies, waits for them, and re-layouts  11.3 us
    pallas_call x1, Pallas kernels, sums(): pl.pallas_call(functools.partial(sums_kernel, n, m), out_shape=(shape(dbc...  8.75 us

profile of v3, /device:TPU:0, one launch (start us, length us, event | category | flops | bytes accessed | tf_op | source)
XLA Modules:
  0.0 114.6 jit_solution(2812143985668899566)
XLA Ops:
  0.6 0.8 copy.17
  1.4 0.2 reduce_window_sum.11
  1.6 0.0 copy-start.18
  1.6 0.1 broadcast_in_dim.6.dec_ref.dec
  1.7 0.0 copy-start.16
  1.7 0.1 copy.18
  1.8 0.0 copy-start.12
  1.8 0.7 copy-done.18
  2.4 0.0 copy-start.8
  2.4 0.0 copy-start.15
  2.5 0.0 copy-start.19
  2.5 0.7 copy-done.19
  3.2 0.0 copy-done.12
  3.2 0.0 copy-done.16
  3.2 0.0 copy-done.8
  3.2 0.1 copy-done.15
  3.3 0.0 copy-start
  3.3 1.0 copy-done
  4.3 0.0 copy-start.2
  4.3 1.0 copy-done.2
  5.4 22.5 %first.1 = (bf16[16,2048]{1,0:T(8,128)(2,1)S(1)}, bf16[16,256]{1,0:T(8,128)(2,1)S(1)}, bf16[16,256]{1,0:T(8,128)(2,1)S(1)}, bf16[8,128,512]{2,1,0:T(8,128)(2,1)S...) custom-call(bf16[128,2048]{1,0:T(8,128)(2,1)S(1)} %copy-done.2, ...), custom_call_target="tpu_custom_call" | custom-call | tf_op jit(solution)/shard_map/first/pallas_call | solution.py:239
  27.9 0.0 copy-start.13
  27.9 0.6 copy-done.13
  28.5 0.6 copy-done.14
  29.1 0.0 copy-done.1
  29.1 0.0 copy-done.7
  29.1 51.6 %chain.1 = (bf16[16,128,128]{2,1,0:T(8,128)(2,1)S(1)}, bf16[16,128,128]{2,1,0:T(8,128)(2,1)S(1)}, f32[128,2048]{1,0:T(8,128)S(1)}, f32[128,2048]{1,0:T(8,128)S(1...) custom-call(f32[8,128,128]{2,1,0:T(8,128)S(1)} %get-tuple-element.48.of, f32[8,128,128]{2,1,0:T(8,128)S(1)} %get-tuple-element.49.ob, ...), custom_call_target="tpu_custom_call" | custom-call | tf_op jit(solution)/shard_map/chain/pallas_call | solution.py:453
  80.7 0.0 copy-start.3
  80.7 1.0 copy-done.3
  81.7 1.0 copy-done.4
  82.7 0.8 copy-done.5
  83.5 0.8 copy-done.6
  84.3 0.7 copy-done.10
  84.9 0.6 copy-done.11
  85.6 0.7 copy-done.20
  86.2 0.7 broadcast_in_dim.7.skip_ref
  86.9 13.9 %ssd.1 = (bf16[128,2048]{1,0:T(8,128)(2,1)}, f32[128,2048]{1,0:T(8,128)}, bf16[16,2048]{1,0:T(8,128)(2,1)}, f32[16,1,128]{2,1,0:T(1,128)}, bf16[128,256]{1,0:T(8...) custom-call(bf16[128,2048]{1,0:T(8,128)(2,1)} %x_ref.3, bf16[16,2048]{1,0:T(8,128)(2,1)} %copy-done.13, ...), custom_call_target="tpu_custom_call" | custom-call | tf_op jit(solution)/shard_map/ssd/pallas_call | solution.py:551
  100.8 8.8 %sums.1 = (f32[128,256]{1,0:T(8,128)}, f32[16,256]{1,0:T(8,128)}, bf16[16,2048]{1,0:T(8,128)(2,1)}) custom-call(bf16[128,256]{1,0:T(8,128)(2,1)} %get-tuple-element.65.bc_ref, bf16[16,2048]{1,0:T(8,128)(2,1)} %get-tuple-element.66.gh_ref), custom_call_target="tpu_custom_call" | custom-call | tf_op jit(solution)/shard_map/sums/pallas_call | solution.py:642
  109.6 0.0 copy-start.17
  109.6 0.7 slice.102
  110.3 0.1 copy-done.17
  110.5 0.1 maximum_multiply_fusion
  110.6 0.1 fusion.3
  110.7 0.7 reshape.71
  111.4 0.8 slice_convert_fusion
  112.2 0.0 copy-done.9
  112.2 0.9 fusion.10
  113.1 1.5 %scatter-add.4 = f32[128,2048]{1,0:T(8,128)} dynamic-update-slice(f32[128,2048]{1,0:T(8,128)} %get-tuple-element.64, f32[3,2048]{1,0:T(4,128)S(1)} %fusion.10, s32[]{:T(128)} %constant.33.clone.1, s32[]{:T(128)} %constant.34.clone.1) | dynamic-update-slice | bytes 49156 | tf_op jit(solution)/shard_map/scatter-add | solution.py:680
  (20 shorter events, 0.1 us)
Async XLA Ops:
  1.6 0.8 copy-start.18
  1.7 1.5 %copy-start.16 = (bf16[128,256]{1,0:T(8,128)(2,1)S(1)}, bf16[128,256]{1,0:T(8,128)(2,1)}, u32[]{:S(2)}) copy-start(bf16[128,256]{1,0:T(8,128)(2,1)} %v_ref.1) | copy-start | bytes 196612
  1.8 1.4 %copy-start.12 = (f32[128,16]{0,1:T(8,128)}, f32[128,16]{0,1:T(8,128)S(1)}, u32[]{:S(2)}) copy-start(f32[128,16]{0,1:T(8,128)S(1)} %copy.18) | copy-start | bytes 24580
  2.4 0.7 copy-start.8
  2.4 0.9 copy-start.15
  2.5 0.7 copy-start.19
  3.3 1.0 copy-start
  4.3 1.0 copy-start.2
  5.4 23.8 %copy-start.1 = (bf16[128,2048]{1,0:T(8,128)(2,1)S(1)}, bf16[128,2048]{1,0:T(8,128)(2,1)}, u32[]{:S(2)}) copy-start(bf16[128,2048]{1,0:T(8,128)(2,1)} %dm_ref.5) | copy-start | bytes 1572868
  5.4 23.8 %copy-start.7 = (bf16[128,2048]{1,0:T(8,128)(2,1)S(1)}, bf16[128,2048]{1,0:T(8,128)(2,1)}, u32[]{:S(2)}) copy-start(bf16[128,2048]{1,0:T(8,128)(2,1)} %q_ref.1) | copy-start | bytes 1572868
  27.9 0.6 copy-start.13
  28.5 0.6 copy-start.14
  80.7 1.0 copy-start.3
  81.7 1.0 copy-start.4
  82.7 0.8 copy-start.5
  83.5 0.8 copy-start.6
  84.3 0.7 copy-start.10
  84.9 0.6 copy-start.11
  85.6 0.7 copy-start.20
  109.6 0.9 copy-start.17
  111.4 0.8 copy-start.9

commit v4 on v3

--- a/solution.py
+++ b/solution.py
@@ -258,8 +258,9 @@
 
 
 def chain_kernel(n, size, of, ob, rf, rb, dec, rdec, kva, q_ref, dm_ref,
-                 s_in, g_in, att_ref, dq_ref, dk_out, dv_out,
-                 af, ab, sf, sb, mf, mb, kt, vt, dka, dva, part, land,
+                 x_ref, xh_ref, w_ref, bcv_ref, run_ref, skip_ref,
+                 dq_ref, dk_out, dv_out, mixed_ref, dx_ref, gh_ref, dla_ref, dbc_ref,
+                 s_in, g_in, att_ref, inner, dinner, dbc, af, ab, sf, sb, mf, mb, kt, vt, dka, dva, part, land,
                  fs, fr, bs, br, mfs, mfr, mbs, mbr, ps, pr):
     me = lax.axis_index("seq")
     share = of.shape[0]
@@ -420,6 +421,67 @@
         return carry
 
     lax.fori_loop(0, chunks, drain, 0)
+    b = bcv_ref[:, :D]
+    c = bcv_ref[:, D:]
+    inner[...] = mm_nt(c, b)
+    dinner[...] = jnp.zeros_like(dinner)
+    dbc[...] = jnp.zeros_like(dbc)
+
+    def ssd(h, carry):
+        lanes = pl.ds(pl.multiple_of(h * D, D), D)
+        dm = dm_ref[:, lanes]
+        dmf = dm.astype(F32)
+        w = w_ref[:, lanes].astype(F32)
+        pre = conv(x_ref[:, lanes].astype(F32), xh_ref[:, lanes].astype(F32), w)
+        sig = sigmoid(pre)
+        xb = (pre * sig).astype(BF16)
+        xf = xb.astype(F32)
+        row = run_ref[h]
+        col = columns(row)
+        final = row[:, rows - 1:]
+        t_i = lax.broadcasted_iota(jnp.int32, (rows, rows), 0)
+        s_i = lax.broadcasted_iota(jnp.int32, (rows, rows), 1)
+        fade = jnp.exp(jnp.where(t_i >= s_i, col - row, -1e30))
+        mix = inner[...] * fade
+        skip = skip_ref[h]
+        enter = jnp.exp(col)
+        tail = jnp.exp(final - col)
+        state = s_in[h]
+        grad = g_in[h]
+        carried = enter * mm(c, state)
+        y = mm(mix.astype(BF16), xb) + carried + skip * xf
+        mixed_ref[:, lanes] = (y + att_ref[:, lanes]).astype(BF16)
+        back = tail * mm(b, grad)
+        gx = mm(jnp.transpose(mix).astype(BF16), dm) + back + skip * dmf
+        dmix = mm_nt(dm, xb)
+        dinner[...] += dmix * fade
+        dbc[:, D:] += mm_nt((enter * dmf).astype(BF16), state)
+        dbc[:, :D] += mm_nt((tail * xf).astype(BF16), grad)
+        dgap = dmix * mix
+        away = xf * back
+        net = dgap - jnp.transpose(dgap) + dmf * carried - away
+        net = jnp.sum(net, axis=1, keepdims=True)
+        dfinal = jnp.sum(away) + jnp.sum(
+            jnp.exp(final) * jnp.sum(state.astype(F32) * grad.astype(F32), axis=0, keepdims=True))
+        dla_ref[h] = jnp.sum(jnp.where(t_i >= s_i, net, 0.0), axis=0, keepdims=True) + dfinal
+
+        g = gx * (sig * (1.0 + pre * (1.0 - sig)))
+        gh_ref[:, lanes] = g[:EDGE].astype(BF16)
+        width = w.shape[0]
+        padded = jnp.concatenate([g, jnp.zeros((8, D), F32)], axis=0)
+        total = None
+        for tap in range(width):
+            offset = width - 1 - tap
+            term = w[tap:tap + 1] * padded[offset:offset + rows]
+            total = term if total is None else total + term
+        dx_ref[:, lanes] = total
+        return carry
+
+    lax.fori_loop(0, heads, ssd, 0)
+    di = dinner[...]
+    dbc_ref[:, D:] = (dbc[:, D:] + mm(di.astype(BF16), b)).astype(BF16)
+    dbc_ref[:, :D] = (dbc[:, :D] + mm(jnp.transpose(di).astype(BF16), c)).astype(BF16)
+
     for kv in range(kv_heads):
         cols = slice(kv * D, kv * D + D)
         own = part[kv, me].astype(F32)
@@ -440,7 +502,8 @@
                 lend(kv, off, lax.rem(me - off + n, n)).wait_send()
 
 
-def chain(n, of, ob, rf, rb, dec, rdec, kva, queries, d_mixed):
+def chain(n, of, ob, rf, rb, dec, rdec, kva, queries, d_mixed, x_in, xh, conv_x, bcv, run_rows,
+          skip_rows):
     share = of.shape[0]
     rows, wide = queries.shape
     width = kva.shape[2] // 2
@@ -449,14 +512,17 @@
     chunks = share // size
     dma = pltpu.SemaphoreType.DMA
     shape = jax.ShapeDtypeStruct
-    out = shape((2 * share, D, D), BF16)
+    states = pltpu.VMEM((2 * share, D, D), BF16)
     return pl.pallas_call(
         functools.partial(chain_kernel, n, size),
-        out_shape=(out, out, shape((rows, wide), F32), shape((rows, wide), F32),
-                   shape((rows, width), F32), shape((rows, width), F32)),
-        in_specs=[VMEM] * 9,
-        out_specs=(VMEM,) * 6,
+        out_shape=(shape((rows, wide), F32), shape((rows, width), F32), shape((rows, width), F32),
+                   shape((rows, wide), BF16), shape((rows, wide), F32), shape((EDGE, wide), BF16),
+                   shape((2 * share, 1, rows), F32), shape(bcv.shape, BF16)),
+        in_specs=[VMEM] * 15,
+        out_specs=(VMEM,) * 8,
         scratch_shapes=[
+            states, states, pltpu.VMEM((rows, wide), F32), pltpu.VMEM((rows, rows), F32),
+            pltpu.VMEM((rows, rows), F32), pltpu.VMEM(bcv.shape, F32),
             *[pltpu.VMEM(of.shape, BF16) for _ in range(6)],
             pltpu.VMEM((D, n * rows), BF16), pltpu.VMEM((D, n * rows), BF16),
             pltpu.VMEM((n * rows, D), F32), pltpu.VMEM((n * rows, D), F32),
@@ -466,105 +532,7 @@
         compiler_params=pltpu.CompilerParams(
             collective_id=1, has_side_effects=True, vmem_limit_bytes=28 * 2**20),
         name="chain",
-    )(of, ob, rf, rb, dec, rdec, kva, queries, d_mixed)
-
-
-def ssd_kernel(heads, x_ref, xh_ref, w_ref, dm_ref, bcv_ref, run_ref, skip_ref, att_ref, s_ref, g_ref,
-               dqi_ref, dki_ref, dvi_ref, mixed_ref, dx_ref, gh_ref, dla_ref, dbc_ref,
-               dq_ref, dk_ref, dv_ref, inner, dinner, dbc):
-    h = pl.program_id(0)
-    rows = x_ref.shape[0]
-    b = bcv_ref[:, :D]
-    c = bcv_ref[:, D:]
-
-    @pl.when(h == 0)
-    def _():
-        inner[...] = mm_nt(c, b)
-        dinner[...] = jnp.zeros_like(dinner)
-        dbc[...] = jnp.zeros_like(dbc)
-
-    dq_ref[...] = dqi_ref[...]
-    dm = dm_ref[...]
-    dmf = dm.astype(F32)
-    w = w_ref[...].astype(F32)
-    pre = conv(x_ref[...].astype(F32), xh_ref[...].astype(F32), w)
-    sig = sigmoid(pre)
-    xb = (pre * sig).astype(BF16)
-    xf = xb.astype(F32)
-    row = run_ref[0]
-    col = columns(row)
-    final = row[:, rows - 1:]
-    t_i = lax.broadcasted_iota(jnp.int32, (rows, rows), 0)
-    s_i = lax.broadcasted_iota(jnp.int32, (rows, rows), 1)
-    fade = jnp.exp(jnp.where(t_i >= s_i, col - row, -1e30))
-    mix = inner[...] * fade
-    skip = skip_ref[0]
-    enter = jnp.exp(col)
-    tail = jnp.exp(final - col)
-    state = s_ref[0]
-    grad = g_ref[0]
-    carried = enter * mm(c, state)
-    y = mm(mix.astype(BF16), xb) + carried + skip * xf
-    mixed_ref[...] = (y + att_ref[...]).astype(BF16)
-    back = tail * mm(b, grad)
-    gx = mm(jnp.transpose(mix).astype(BF16), dm) + back + skip * dmf
-    dmix = mm_nt(dm, xb)
-    dinner[...] += dmix * fade
-    dbc[:, D:] += mm_nt((enter * dmf).astype(BF16), state)
-    dbc[:, :D] += mm_nt((tail * xf).astype(BF16), grad)
-    dgap = dmix * mix
-    away = xf * back
-    net = dgap - jnp.transpose(dgap) + dmf * carried - away
-    net = jnp.sum(net, axis=1, keepdims=True)
-    dfinal = jnp.sum(away) + jnp.sum(
-        jnp.exp(final) * jnp.sum(state.astype(F32) * grad.astype(F32), axis=0, keepdims=True))
-    dla_ref[0] = jnp.sum(jnp.where(t_i >= s_i, net, 0.0), axis=0, keepdims=True) + dfinal
-
-    g = gx * (sig * (1.0 + pre * (1.0 - sig)))
-    gh_ref[...] = g[:EDGE].astype(BF16)
-    width = w.shape[0]
-    padded = jnp.concatenate([g, jnp.zeros((8, D), F32)], axis=0)
-    total = None
-    for tap in range(width):
-        offset = width - 1 - tap
-        term = w[tap:tap + 1] * padded[offset:offset + rows]
-        total = term if total is None else total + term
-    dx_ref[...] = total
-
-    @pl.when(h == heads - 1)
-    def _():
-        dk_ref[...] = dki_ref[...]
-        dv_ref[...] = dvi_ref[...]
-        di = dinner[...]
-        dbc_ref[:, D:] = (dbc[:, D:] + mm(di.astype(BF16), b)).astype(BF16)
-        dbc_ref[:, :D] = (dbc[:, :D] + mm(jnp.transpose(di).astype(BF16), c)).astype(BF16)
-
-
-def ssd_part(x_in, xh, conv_x, d_mixed, bcv, run_rows, skip_rows, att, s_in, g_in, dq, dk, dv):
-    rows, wide = x_in.shape
-    heads = wide // D
-    by_head = lambda r: pl.BlockSpec((r, D), lambda h: (0, h))
-    whole = lambda a: pl.BlockSpec(a.shape, lambda h: (0,) * a.ndim)
-    cube = pl.BlockSpec((1, D, D), lambda h: (h, 0, 0))
-    line = lambda r: pl.BlockSpec((1, 1, r), lambda h: (h, 0, 0))
-    shape = jax.ShapeDtypeStruct
-    return pl.pallas_call(
-        functools.partial(ssd_kernel, heads),
-        grid=(heads,),
-        out_shape=(
-            shape((rows, wide), BF16), shape((rows, wide), F32), shape((EDGE, wide), BF16),
-            shape((heads, 1, rows), F32), shape(bcv.shape, BF16), shape((rows, wide), F32),
-            shape(dk.shape, F32), shape(dv.shape, F32),
-        ),
-        in_specs=[by_head(rows), by_head(EDGE), by_head(conv_x.shape[0]), by_head(rows), whole(bcv),
-                  line(rows), line(D), by_head(rows), cube, cube, by_head(rows), whole(dk),
-                  whole(dv)],
-        out_specs=(by_head(rows), by_head(rows), by_head(EDGE), line(rows), whole(bcv),
-                   by_head(rows), whole(dk), whole(dv)),
-        scratch_shapes=[pltpu.VMEM((rows, rows), F32), pltpu.VMEM((rows, rows), F32),
-                        pltpu.VMEM(bcv.shape, F32)],
-        name="ssd",
-    )(x_in, xh, conv_x, d_mixed, bcv, run_rows, skip_rows, att, s_in, g_in, dq, dk, dv)
+    )(of, ob, rf, rb, dec, rdec, kva, queries, d_mixed, x_in, xh, conv_x, bcv, run_rows, skip_rows)
 
 
 def sums_kernel(n, m, bc_ref, gh_ref, bc_out, bcn_out, gn_out, bb, nb, bs, br, ns, nr, hs, hr):
@@ -670,9 +638,9 @@
     skip_rows = jnp.broadcast_to(skip[:, None, None], (heads, 1, D))
     xh, bch, bcn, kva, bcv, of, ob, rf, rb, rdec = first_part(
         n, x_in, bc, keys, values, conv_x, wbc, run_rows, d_mixed, dec)
-    s_in, g_in, att, dq, dk, dv = chain(n, of, ob, rf, rb, dec, rdec, kva, queries, d_mixed)
-    mixed, dx, gh, dla, dbc, dq, d_keys, d_values = ssd_part(
-        x_in, xh, conv_x, d_mixed, bcv, run_rows, skip_rows, att, s_in, g_in, dq, dk, dv)
+    dq, d_keys, d_values, mixed, dx, gh, dla, dbc = chain(
+        n, of, ob, rf, rb, dec, rdec, kva, queries, d_mixed, x_in, xh, conv_x, bcv, run_rows,
+        skip_rows)
     bcs, bca, gn = sums(n, m, dbc, gh)
     wx = conv_x.astype(F32)
     gnf = jnp.concatenate([jnp.zeros((edge, gn.shape[1]), F32), gn[:edge].astype(F32)], axis=0)

time: 116 us -> 101 us (0.87)
  Pallas kernels: 96.7 us -> 84.1 us
    pallas_call x2 -> x1, Pallas kernels: 65.4 us -> 52.8 us  [chain(): pl.pallas_call(functools.partial(chain_kernel, n, size), out_shape=(shape...]
    scatter-add x1, local copies, waits for them, and re-layouts: 1.51 us -> 0.32 us  [shards(): d_x_in = dx.at[rows - edge:].add(fix)]
    unnamed x44 -> x36, local copies, waits for them, and re-layouts: 11.3 us -> 12.1 us
where the time goes in v4:
time: 101 us; the launch traced here: 100 us
  Pallas kernels  84.1 us (83%)
  local copies, waits for them, and re-layouts  14.1 us (14%)
  other arithmetic  1.2 us (1%)
    pallas_call x1, Pallas kernels, chain(): pl.pallas_call(functools.partial(chain_kernel, n, size), out_shape=(shape...  52.8 us
    pallas_call x1, Pallas kernels, first_part(): pl.pallas_call(functools.partial(first_kernel, n), out_shape=(shape((EDGE...  22.5 us
    unnamed x36, local copies, waits for them, and re-layouts  12.1 us
    pallas_call x1, Pallas kernels, sums(): pl.pallas_call(functools.partial(sums_kernel, n, m), out_shape=(shape(dbc...  8.75 us

profile of v4, /device:TPU:0, one launch (start us, length us, event | category | flops | bytes accessed | tf_op | source)
XLA Modules:
  0.0 100.2 jit_solution(4792711247900000929)
XLA Ops:
  0.6 0.8 copy.17
  1.4 0.2 reduce_window_sum.11
  1.6 0.0 copy-start.11
  1.6 0.1 broadcast_in_dim.6.dec_ref.dec
  1.7 0.0 copy-start.7
  1.7 0.1 copy.18
  1.8 0.7 copy-done.11
  2.4 0.0 copy-start.5
  2.4 0.0 copy-start.6
  2.5 0.0 copy-start.12
  2.5 0.7 copy-done.12
  3.2 0.0 copy-done.7
  3.2 0.0 copy-done.5
  3.2 0.1 copy-done.6
  3.3 0.0 copy-start
  3.3 1.0 %copy-done = bf16[128,2048]{1,0:T(8,128)(2,1)S(1)} copy-done((bf16[128,2048]{1,0:T(8,128)(2,1)S(1)}, bf16[128,2048]{1,0:T(8,128)(2,1)}, u32[]{:S(2)}) %copy-start) | copy-done | bytes 524312
  4.3 0.0 copy-start.2
  4.3 1.0 %copy-done.2 = bf16[128,2048]{1,0:T(8,128)(2,1)S(1)} copy-done((bf16[128,2048]{1,0:T(8,128)(2,1)S(1)}, bf16[128,2048]{1,0:T(8,128)(2,1)}, u32[]{:S(2)}) %copy-start.2) | copy-done | bytes 524312
  5.4 0.0 copy-start.1
  5.4 0.0 copy-start.3
  5.4 22.5 %first.1 = (bf16[16,2048]{1,0:T(8,128)(2,1)S(1)}, bf16[16,256]{1,0:T(8,128)(2,1)S(1)}, bf16[16,256]{1,0:T(8,128)(2,1)S(1)}, bf16[8,128,512]{2,1,0:T(8,128)(2,1)S...) custom-call(bf16[128,2048]{1,0:T(8,128)(2,1)S(1)} %copy-done, ...), custom_call_target="tpu_custom_call" | custom-call | tf_op jit(solution)/shard_map/first/pallas_call | solution.py:239
  27.9 0.0 copy-start.13
  27.9 0.6 copy-done.13
  28.6 0.1 broadcast_in_dim.7.skip_ref
  28.6 0.0 copy-done.1
  28.6 0.0 copy-done.3
  28.6 0.0 copy-start.4
  28.7 1.0 %copy-done.4 = bf16[128,2048]{1,0:T(8,128)(2,1)S(1)} copy-done((bf16[128,2048]{1,0:T(8,128)(2,1)S(1)}, bf16[128,2048]{1,0:T(8,128)(2,1)}, u32[]{:S(2)}) %copy-start.4) | copy-done | bytes 524312
  29.7 52.8 %chain.1 = (f32[128,2048]{1,0:T(8,128)S(1)}, f32[128,256]{1,0:T(8,128)S(1)}, f32[128,256]{1,0:T(8,128)S(1)}, bf16[128,2048]{1,0:T(8,128)(2,1)S(1)}, f32[128,2048...) custom-call(f32[8,128,128]{2,1,0:T(8,128)S(1)} %get-tuple-element.40.of, ...), custom_call_target="tpu_custom_call" | custom-call | tf_op jit(solution)/shard_map/chain/pallas_call | solution.py:516
  82.5 0.0 copy-start.8
  82.6 0.6 copy-done.8
  83.2 0.0 copy-start.9
  83.2 0.6 copy-done.9
  83.8 8.7 %sums.1 = (f32[128,256]{1,0:T(8,128)}, f32[16,256]{1,0:T(8,128)}, bf16[16,2048]{1,0:T(8,128)(2,1)}) custom-call(bf16[128,256]{1,0:T(8,128)(2,1)} %copy-done.9, bf16[16,2048]{1,0:T(8,128)(2,1)} %copy-done.8), custom_call_target="tpu_custom_call" | custom-call | tf_op jit(solution)/shard_map/sums/pallas_call | solution.py:610
  92.6 0.0 copy-start.10
  92.6 0.7 slice.102
  93.4 0.1 copy-done.10
  93.5 0.1 maximum_multiply_fusion
  93.6 0.1 fusion.3
  93.7 0.7 reshape.71
  94.4 0.8 slice_convert_fusion
  95.3 0.3 scatter-add.4
  95.6 0.8 copy.33
  96.4 1.0 copy.34
  97.4 0.7 copy.35
  98.0 0.7 copy.36
  98.7 1.0 copy.37
  99.6 0.6 copy.38
  (11 shorter events, 0.1 us)
Async XLA Ops:
  1.6 0.8 copy-start.11
  1.7 1.5 %copy-start.7 = (bf16[128,256]{1,0:T(8,128)(2,1)S(1)}, bf16[128,256]{1,0:T(8,128)(2,1)}, u32[]{:S(2)}) copy-start(bf16[128,256]{1,0:T(8,128)(2,1)} %v_ref.1) | copy-start | bytes 196612
  2.4 0.7 copy-start.5
  2.4 0.9 copy-start.6
  2.5 0.7 copy-start.12
  3.3 1.0 %copy-start = (bf16[128,2048]{1,0:T(8,128)(2,1)S(1)}, bf16[128,2048]{1,0:T(8,128)(2,1)}, u32[]{:S(2)}) copy-start(bf16[128,2048]{1,0:T(8,128)(2,1)} %x_ref.3) | copy-start | bytes 1572868
  4.3 1.0 %copy-start.2 = (bf16[128,2048]{1,0:T(8,128)(2,1)S(1)}, bf16[128,2048]{1,0:T(8,128)(2,1)}, u32[]{:S(2)}) copy-start(bf16[128,2048]{1,0:T(8,128)(2,1)} %dm_ref.3) | copy-start | bytes 1572868
  5.4 23.2 %copy-start.1 = (bf16[128,2048]{1,0:T(8,128)(2,1)S(1)}, bf16[128,2048]{1,0:T(8,128)(2,1)}, u32[]{:S(2)}) copy-start(bf16[128,2048]{1,0:T(8,128)(2,1)} %x_ref.3) | copy-start | bytes 1572868
  5.4 23.2 %copy-start.3 = (bf16[128,2048]{1,0:T(8,128)(2,1)S(1)}, bf16[128,2048]{1,0:T(8,128)(2,1)}, u32[]{:S(2)}) copy-start(bf16[128,2048]{1,0:T(8,128)(2,1)} %dm_ref.3) | copy-start | bytes 1572868
  27.9 0.7 copy-start.13
  28.6 1.0 %copy-start.4 = (bf16[128,2048]{1,0:T(8,128)(2,1)S(1)}, bf16[128,2048]{1,0:T(8,128)(2,1)}, u32[]{:S(2)}) copy-start(bf16[128,2048]{1,0:T(8,128)(2,1)} %q_ref.1) | copy-start | bytes 1572868
  82.5 0.6 copy-start.8
  83.2 0.6 copy-start.9
  92.6 0.9 copy-start.10

commit v5 on v4

--- a/solution.py
+++ b/solution.py
@@ -377,7 +377,7 @@
         def _():
             part[kv, :, :, :D] = (dka[...] * scale).astype(BF16).reshape(n, rows, D)
             part[kv, :, :, D:] = dva[...].astype(BF16).reshape(n, rows, D)
-            for off in range(1, n):
+            for off in reversed(range(1, n)):
                 @pl.when(me - off >= 0)
                 def _():
                     lend(kv, off, lax.rem(me - off + n, n)).start()
@@ -620,6 +620,44 @@
     )(dbc, gh)
 
 
+def finish_kernel(dqi, mixedi, dxi, gn, w_ref, dki, dvi, dq, mixed, dx, dk, dv):
+    rows = dx.shape[0]
+    taps = w_ref.shape[0]
+    dq[...] = dqi[...]
+    mixed[...] = mixedi[...]
+    w = w_ref[...].astype(F32)
+    after = gn[...].astype(F32)[:8]
+    after = jnp.concatenate([jnp.zeros_like(after), after], axis=0)
+    total = None
+    for tap in range(taps):
+        offset = taps - 1 - tap
+        term = w[tap:tap + 1] * after[offset:offset + 8]
+        total = term if total is None else total + term
+    dx[:rows - 8] = dxi[:rows - 8]
+    dx[rows - 8:] = dxi[rows - 8:] + total
+
+    @pl.when(pl.program_id(0) == 0)
+    def _():
+        dk[...] = dki[...]
+        dv[...] = dvi[...]
+
+
+def finish(dq, mixed, dx, gn, conv_x, dk, dv):
+    rows, wide = dx.shape
+    lanes = math.gcd(512, wide)
+    cols = lambda a: pl.BlockSpec((a.shape[0], lanes), lambda i: (0, i))
+    whole = lambda a: pl.BlockSpec(a.shape, lambda i: (0, 0))
+    like = lambda a: jax.ShapeDtypeStruct(a.shape, a.dtype)
+    return pl.pallas_call(
+        finish_kernel,
+        grid=(wide // lanes,),
+        out_shape=(like(dq), like(mixed), like(dx), like(dk), like(dv)),
+        in_specs=[cols(dq), cols(mixed), cols(dx), cols(gn), cols(conv_x), whole(dk), whole(dv)],
+        out_specs=(cols(dq), cols(mixed), cols(dx), whole(dk), whole(dv)),
+        name="finish",
+    )(dq, mixed, dx, gn, conv_x, dk, dv)
+
+
 def silu_slope(pre):
     s = jax.nn.sigmoid(pre)
     return s * (1.0 + pre * (1.0 - s))
@@ -642,10 +680,7 @@
         n, of, ob, rf, rb, dec, rdec, kva, queries, d_mixed, x_in, xh, conv_x, bcv, run_rows,
         skip_rows)
     bcs, bca, gn = sums(n, m, dbc, gh)
-    wx = conv_x.astype(F32)
-    gnf = jnp.concatenate([jnp.zeros((edge, gn.shape[1]), F32), gn[:edge].astype(F32)], axis=0)
-    fix = sum(wx[j] * gnf[edge - j:2 * edge - j] for j in range(taps))
-    d_x_in = dx.at[rows - edge:].add(fix)
+    dq, mixed, d_x_in, d_keys, d_values = finish(dq, mixed, dx, gn, conv_x, d_keys, d_values)
     wb = wbc.astype(F32)
     full = jnp.concatenate([bch[EDGE - edge:], bc, bcn[:edge]], axis=0).astype(F32)
     pre = sum(wb[j] * full[j:j + rows + edge] for j in range(taps))

time: 101 us -> 105 us (1.040)
  Pallas kernels: 84.1 us -> 89.4 us
    pallas_call x0 -> x1, Pallas kernels: none -> 4.31 us  [finish(): pl.pallas_call(finish_kernel, grid=(wide // lanes,), out_shape=(like(dq),...]
    unnamed x36 -> x41, local copies, waits for them, and re-layouts: 12.1 us -> 12.2 us
where the time goes in v5:
time: 105 us; the launch traced here: 104 us
  Pallas kernels  89.4 us (85%)
  local copies, waits for them, and re-layouts  13.8 us (13%)
    pallas_call x1, Pallas kernels, chain(): pl.pallas_call(functools.partial(chain_kernel, n, size), out_shape=(shape...  53.8 us
    pallas_call x1, Pallas kernels, first_part(): pl.pallas_call(functools.partial(first_kernel, n), out_shape=(shape((EDGE...  22.5 us
    unnamed x41, local copies, waits for them, and re-layouts  12.2 us
    pallas_call x1, Pallas kernels, sums(): pl.pallas_call(functools.partial(sums_kernel, n, m), out_shape=(shape(dbc...  8.74 us
    pallas_call x1, Pallas kernels, finish(): pl.pallas_call(finish_kernel, grid=(wide // lanes,), out_shape=(like(dq),...  4.31 us

profile of v5, /device:TPU:0, one launch (start us, length us, event | category | flops | bytes accessed | tf_op | source)
XLA Modules:
  0.0 104.4 jit_solution(2202213172312256989)
XLA Ops:
  0.6 0.8 copy.17
  1.4 0.2 reduce_window_sum.11
  1.6 0.0 copy-start.16
  1.6 0.1 broadcast_in_dim.4.dec_ref.dec
  1.7 0.0 copy-start.12
  1.7 0.1 copy.18
  1.8 0.7 copy-done.16
  2.4 0.0 copy-start.11
  2.5 0.0 copy-start.17
  2.5 0.7 copy-done.17
  3.2 0.0 copy-done.12
  3.2 0.0 copy-done.8
  3.2 0.1 copy-done.11
  3.3 0.0 copy-start
  3.3 1.0 copy-done
  4.3 0.0 copy-start.2
  4.3 1.0 copy-done.2
  5.4 0.0 copy-start.1
  5.4 0.0 copy-start.3
  5.4 22.5 %first.1 = (bf16[16,2048]{1,0:T(8,128)(2,1)S(1)}, bf16[16,256]{1,0:T(8,128)(2,1)S(1)}, bf16[16,256]{1,0:T(8,128)(2,1)S(1)}, bf16[8,128,512]{2,1,0:T(8,128)(2,1)S...) custom-call(bf16[128,2048]{1,0:T(8,128)(2,1)S(1)} %copy-done, ...), custom_call_target="tpu_custom_call" | custom-call | tf_op jit(solution)/shard_map/first/pallas_call | solution.py:239
  27.9 0.0 copy-start.18
  27.9 0.6 copy-done.18
  28.6 0.1 broadcast_in_dim.5.skip_ref
  28.6 0.0 copy-done.1
  28.6 0.0 copy-done.3
  28.6 0.0 copy-start.6
  28.7 1.0 copy-done.6
  29.7 53.8 %chain.1 = (f32[128,2048]{1,0:T(8,128)S(1)}, f32[128,256]{1,0:T(8,128)S(1)}, f32[128,256]{1,0:T(8,128)S(1)}, bf16[128,2048]{1,0:T(8,128)(2,1)S(1)}, f32[128,2048...) custom-call(f32[8,128,128]{2,1,0:T(8,128)S(1)} %get-tuple-element.33.of, ...), custom_call_target="tpu_custom_call" | custom-call | tf_op jit(solution)/shard_map/chain/pallas_call | solution.py:516
  83.5 0.0 copy-start.4
  83.5 1.0 copy-done.4
  84.5 0.0 copy-start.5
  84.5 1.0 copy-done.5
  85.5 0.0 copy-start.7
  85.5 0.8 copy-done.7
  86.3 0.0 copy-start.9
  86.3 0.7 copy-done.9
  87.0 0.7 copy-done.10
  87.6 0.6 copy-done.13
  88.2 0.6 copy-done.14
  88.9 8.7 %sums.1 = (f32[128,256]{1,0:T(8,128)}, f32[16,256]{1,0:T(8,128)}, bf16[16,2048]{1,0:T(8,128)(2,1)}) custom-call(bf16[128,256]{1,0:T(8,128)(2,1)} %copy-done.14, bf16[16,2048]{1,0:T(8,128)(2,1)} %copy-done.13), custom_call_target="tpu_custom_call" | custom-call | tf_op jit(solution)/shard_map/sums/pallas_call | solution.py:610
  97.6 0.0 copy-start.15
  97.6 0.7 slice.54
  98.4 0.1 copy-done.15
  98.5 0.1 maximum_multiply_fusion
  98.7 0.1 fusion.3
  98.7 0.7 reshape.43
  99.4 4.3 %finish.1 = (f32[128,2048]{1,0:T(8,128)}, bf16[128,2048]{1,0:T(8,128)(2,1)}, f32[128,2048]{1,0:T(8,128)}, f32[128,256]{1,0:T(8,128)}, f32[128,256]{1,0:T(8,128)}) custom-call(f32[128,2048]{1,0:T(8,128)} %copy-done.4, bf16[128,2048]{1,0:T(8,128)(2,1)} %copy-done.7, f32[128,2048]{1,0:T(8,128)} %copy-done.5, bf16[16,2048]{1,0:T(8,128)(2,1)} %get-tuple-element.46.gn, ...), custom_call_target="tpu_custom_call" | custom-call | tf_op jit(solution)/shard_map/finish/pallas_call | solution.py:651
  103.8 0.6 copy.27
  (11 shorter events, 0.1 us)
Async XLA Ops:
  1.6 0.8 copy-start.16
  1.7 1.5 %copy-start.12 = (bf16[128,256]{1,0:T(8,128)(2,1)S(1)}, bf16[128,256]{1,0:T(8,128)(2,1)}, u32[]{:S(2)}) copy-start(bf16[128,256]{1,0:T(8,128)(2,1)} %v_ref.1) | copy-start | bytes 196612
  2.4 0.7 copy-start.8
  2.4 0.9 copy-start.11
  2.5 0.7 copy-start.17
  3.3 1.0 copy-start
  4.3 1.0 copy-start.2
  5.4 23.2 %copy-start.1 = (bf16[128,2048]{1,0:T(8,128)(2,1)S(1)}, bf16[128,2048]{1,0:T(8,128)(2,1)}, u32[]{:S(2)}) copy-start(bf16[128,2048]{1,0:T(8,128)(2,1)} %x_ref.3) | copy-start | bytes 1572868
  5.4 23.2 %copy-start.3 = (bf16[128,2048]{1,0:T(8,128)(2,1)S(1)}, bf16[128,2048]{1,0:T(8,128)(2,1)}, u32[]{:S(2)}) copy-start(bf16[128,2048]{1,0:T(8,128)(2,1)} %dm_ref.3) | copy-start | bytes 1572868
  27.9 0.7 copy-start.18
  28.6 1.0 %copy-start.6 = (bf16[128,2048]{1,0:T(8,128)(2,1)S(1)}, bf16[128,2048]{1,0:T(8,128)(2,1)}, u32[]{:S(2)}) copy-start(bf16[128,2048]{1,0:T(8,128)(2,1)} %q_ref.1) | copy-start | bytes 1572868
  83.5 1.0 copy-start.4
  84.5 1.0 copy-start.5
  85.5 0.8 copy-start.7
  86.3 0.7 copy-start.9
  87.0 0.7 copy-start.10
  87.6 0.6 copy-start.13
  88.2 0.6 copy-start.14
  97.6 0.9 copy-start.15
